TPU v7x, 32 devices: a whole 2x2x4 slice. The times are simulated.
32 devices in a mesh: groups: 2 (over x), wide: 16 (over z, y, core).
Axes of the slice: x: 2, y: 2, z: 4, core: 2. Of those that a mesh axis runs over, the one named last changes fastest.
Arguments:
- hidden_states: bfloat16 [2048, 64, 1024], P(('groups', 'wide')), parts along dimension 0, may hold values from -6 to 6
- block_owner: int32 [2048, 1], P(('groups', 'wide')), parts along dimension 0, may hold values from 0 to 15; in each aligned block of 64 rows (0 to 63, 64 to 127, ...) at most 8 rows name the same one
- token_doc: int32 [2048, 64], P(('groups', 'wide')), parts along dimension 0, may hold values from 0 to 7, never falling along the last dimension, each value on 1 to 32 neighbouring positions
- token_live: int32 [2048, 64], P(('groups', 'wide')), parts along dimension 0, may hold values 0 or 1
- proj_weight: bfloat16 [1024, 128], replicated, may hold values from -0.1875 to 0.1875
- queries: bfloat16 [2048, 128], P(('groups', 'wide')), parts along dimension 0, may hold values from -1.5 to 1.5
Outputs:
- scores: float32 [256, 1024], P(('groups', 'wide')), parts along dimension 0
There are 2 independent parts, one for each index of `groups`. A program takes and returns all parts, laid end to end along the dimension named above; an argument that names none is the same for every part. Nothing has to cross between parts.
Inputs may be any that keep to these rules, and one draw needn't show every extreme that they name: `block_owner`: among the 64 blocks of one index of wide no owner is named by more than 8 blocks, a bound that some block reaches. `token_doc`: within a block the ids never fall and every id appears.
All inputs are finite; a program needn't handle non-finite values. No bound on the sum of `token_live` on one device may be relied on, other than what follows from the above.
Results may differ from a plain program's by a relative error of at most 0.0011.
Values may be sent and summed in bfloat16 or wider, within the bound.
No kernel may reach another device: no remote copies, remote signals or barrier semaphores. Data moves between devices by JAX's collectives and lax.ppermute only.
A program may use at most 64 MiB of HBM per device.

v0:
```python
import functools

import jax
import jax.numpy as jnp
from jax import lax
from jax.experimental import pallas as pl
from jax.experimental.pallas import tpu as pltpu
from jax.sharding import PartitionSpec as P


DOC_DEV = 8
CHUNK = 8
GROUP = 8
UNROLL = 16
LOW = -1000000000.0
PARTS = (3, 3, 2)

VMEM = pl.BlockSpec(memory_space=pltpu.VMEM)
PARAMS = pltpu.CompilerParams(vmem_limit_bytes=24 << 20)


def bit_reverse(value, bits):
    out = value * 0
    for bit in range(bits):
        out = out | (((value >> bit) & 1) << (bits - 1 - bit))
    return out


def pack_kernel(
    h_hbm, w_hbm, doc_hbm, live_hbm, out_ref, meta_ref, h_ref, w_ref, doc_ref, live_ref, sems, *, start
):
    nb, bl, d = h_ref.shape
    dim = w_ref.shape[1]
    small = [
        pltpu.make_async_copy(w_hbm, w_ref, sems.at[0]),
        pltpu.make_async_copy(doc_hbm.at[pl.ds(start, nb)], doc_ref, sems.at[1]),
        pltpu.make_async_copy(live_hbm.at[pl.ds(start, nb)], live_ref, sems.at[2]),
    ]
    large = [
        pltpu.make_async_copy(
            h_hbm.at[pl.ds(start + g * GROUP, GROUP)], h_ref.at[pl.ds(g * GROUP, GROUP)], sems.at[3 + g]
        )
        for g in range(nb // GROUP)
    ]
    for copy in small + large:
        copy.start()
    for copy in small[1:]:
        copy.wait()
    sub = lax.broadcasted_iota(jnp.int32, (8, bl), 0)
    earlier = (
        lax.broadcasted_iota(jnp.int32, (8, 8), 0) > lax.broadcasted_iota(jnp.int32, (8, 8), 1)
    ).astype(jnp.float32)
    doc = doc_ref[...]
    live = live_ref[...] == 1
    livef = live.astype(jnp.float32)
    upto = lax.broadcasted_iota(jnp.int32, (bl, bl), 0) <= lax.broadcasted_iota(
        jnp.int32, (bl, bl), 1
    )
    counted = jnp.dot(livef, upto.astype(jnp.float32), preferred_element_type=jnp.float32)
    before = jnp.zeros((nb, bl), jnp.float32)
    extra = jnp.zeros((nb, bl), jnp.int32)
    for slot in range(DOC_DEV):
        n = jnp.sum(jnp.where(doc == slot, livef, 0.0), axis=1, keepdims=True)
        more = jnp.maximum((n.astype(jnp.int32) - 1) >> 3, 0)
        before = before + jnp.where(doc > slot, n, 0.0)
        extra = extra + jnp.where(doc > slot, more, 0)
    rank = (counted - livef - before).astype(jnp.int32)
    part, group = rank >> 3, rank & 7
    row = jnp.where(part == 0, group * 8 + doc, 64 + group * 8 + extra + part - 1)
    row = jnp.where(live, row, -1)
    live_doc = jnp.where(live, doc, -1)
    small[0].wait()
    for g in range(nb // GROUP):
        large[g].wait()
        projected = jnp.dot(
            h_ref[g * GROUP : (g + 1) * GROUP].reshape(GROUP * bl, d),
            w_ref[...],
            preferred_element_type=jnp.float32,
        )
        total = jnp.sum(projected * projected, axis=1, keepdims=True)
        vectors = (projected * lax.rsqrt(total + 1e-06)).astype(jnp.bfloat16)
        for u in range(GROUP):
            b = g * GROUP + u
            tiles, counts = [], []
            for tile in range(2):
                hits = [
                    (row[b : b + 1] == sub + (64 * tile + 8 * g8)).astype(jnp.float32)
                    for g8 in range(CHUNK)
                ]
                count = jnp.sum(functools.reduce(jnp.add, hits), axis=1, keepdims=True)
                counts.append(count)
                tiles += hits[:1]
                tiles += [jnp.where(count > float(i), hits[i], hits[0]) for i in range(1, CHUNK)]
            pick = jnp.concatenate(tiles, axis=0).astype(jnp.bfloat16)
            out_ref[b] = jnp.dot(
                pick, vectors[u * bl : (u + 1) * bl], preferred_element_type=jnp.float32
            ).astype(jnp.bfloat16)
            n = jnp.sum((live_doc[b : b + 1] == sub).astype(jnp.float32), axis=1, keepdims=True)
            n = jnp.broadcast_to(n, (8, dim)).astype(jnp.int32)
            more = jnp.maximum((n - 1) >> 3, 0)
            first = jnp.dot(
                earlier, more.astype(jnp.float32), preferred_element_type=jnp.float32
            ).astype(jnp.int32)
            for tile in range(2):
                meta_ref[b, tile] = jnp.broadcast_to((counts[tile] > 0).astype(jnp.int32), (8, dim))
            for j in range(3):
                meta_ref[b, 2 + j] = jnp.where(more > j, first + j, 7)


def pack(hidden_states, proj_weight, token_doc, token_live, start, nb):
    bl, d = hidden_states.shape[1:]
    dim = proj_weight.shape[1]
    return pl.pallas_call(
        functools.partial(pack_kernel, start=start),
        in_specs=[pl.BlockSpec(memory_space=pltpu.HBM)] * 4,
        out_specs=[VMEM, VMEM],
        out_shape=[
            pltpu.VMEM((nb, 128, dim), jnp.bfloat16),
            pltpu.VMEM((nb, 5, 8, dim), jnp.int32),
        ],
        scratch_shapes=[
            pltpu.VMEM((nb, bl, d), hidden_states.dtype),
            pltpu.VMEM((d, dim), proj_weight.dtype),
            pltpu.VMEM((nb, bl), jnp.int32),
            pltpu.VMEM((nb, bl), jnp.int32),
            pltpu.SemaphoreType.DMA((3 + nb // GROUP,)),
        ],
        cost_estimate=pl.CostEstimate(
            flops=2 * nb * bl * d * dim, bytes_accessed=2 * nb * bl * d, transcendentals=nb * bl
        ),
        compiler_params=PARAMS,
        name="pack",
    )(*(in_hbm(x) for x in (hidden_states, proj_weight, token_doc, token_live)))


def score_kernel(owner_ref, *refs, parts, width):
    vec_refs, meta_refs, got_ref = refs[:parts], refs[parts : 2 * parts], refs[2 * parts]
    keep_ref, send_ref, query_ref, table_ref = refs[2 * parts + 1 :]
    n = lax.axis_size("wide")
    bits = n.bit_length() - 1
    me = lax.axis_index("wide")
    columns = got_ref.shape[0]
    piece = columns // (n // 2)
    for j in range(n // 2):
        chip = (me >> 1) ^ bit_reverse(j, bits - 1)
        query_ref[pl.ds(pl.multiple_of(chip * piece, piece), piece), :] = got_ref[
            j * piece : (j + 1) * piece, :
        ]
    table_ref[...] = jnp.full(table_ref.shape, LOW, jnp.float32)
    span = min(columns, 512)

    def visit(vec_ref, meta_ref, b, offset, start):
        place = bit_reverse(owner_ref[offset + b] ^ me, bits)
        rows = pl.ds(pl.multiple_of(place * DOC_DEV, DOC_DEV), DOC_DEV)
        some = [meta_ref[b, tile] > 0 for tile in range(2)]
        index = [meta_ref[b, 2 + j] for j in range(3)]
        tokens = vec_ref[b]
        for t in range(span // width):
            at = pl.ds(start + t * width, width)
            similar = lax.dot_general(
                tokens,
                query_ref[at, :],
                (((1,), (1,)), ((), ())),
                preferred_element_type=jnp.float32,
            )
            first, rest = (
                functools.reduce(
                    jnp.maximum,
                    [similar[64 * tile + 8 * g : 64 * tile + 8 * g + 8] for g in range(CHUNK)],
                )
                for tile in range(2)
            )
            best = []
            for c in range(width // 128):
                top = jnp.where(some[0], first[:, c * 128 : (c + 1) * 128], LOW)
                further = jnp.where(some[1], rest[:, c * 128 : (c + 1) * 128], LOW)
                for j in range(3):
                    top = jnp.maximum(top, jnp.take_along_axis(further, index[j], axis=0))
                best.append(top)
            table_ref[rows, at] = jnp.maximum(table_ref[rows, at], jnp.concatenate(best, axis=1))

    def over_blocks(start):
        offset = 0
        for vec_ref, meta_ref in zip(vec_refs, meta_refs):
            nb = vec_ref.shape[0]
            step = next(s for s in (UNROLL, 12, 8, 4, 2, 1) if nb % s == 0)

            def some_blocks(i, carry, vec_ref=vec_ref, meta_ref=meta_ref, offset=offset, step=step):
                for u in range(step):
                    visit(vec_ref, meta_ref, i * step + u, offset, start)
                return carry

            lax.fori_loop(0, nb // step, some_blocks, 0)
            offset += nb

    if columns == span:
        over_blocks(0)
    else:

        def one_span(i, carry):
            over_blocks(pl.multiple_of(i * span, span))
            return carry

        lax.fori_loop(0, columns // span, one_span, 0)
    half = table_ref.shape[0] // 2
    keep_ref[...] = table_ref[:half, :]
    send_ref[...] = table_ref[half:, :]


def score(owner, packed, meta, gathered, owners):
    dim = gathered.shape[1]
    columns = gathered.shape[0]
    rows = sum(p.shape[0] * p.shape[1] for p in packed)
    half = pltpu.VMEM((owners * DOC_DEV // 2, columns), jnp.float32)
    return pl.pallas_call(
        functools.partial(score_kernel, parts=len(packed), width=256),
        in_specs=[pl.BlockSpec(memory_space=pltpu.SMEM)] + [VMEM] * (2 * len(packed) + 1),
        out_specs=[VMEM, VMEM],
        out_shape=[half, half],
        scratch_shapes=[
            pltpu.VMEM((columns, dim), jnp.bfloat16),
            pltpu.VMEM((owners * DOC_DEV, columns), jnp.float32),
        ],
        cost_estimate=pl.CostEstimate(
            flops=2 * rows * dim * columns, bytes_accessed=4 * rows * dim, transcendentals=0
        ),
        compiler_params=PARAMS,
    )(owner, *packed, *meta, in_vmem(gathered))


def in_hbm(x):
    return pltpu.with_memory_space_constraint(x, pltpu.HBM)


def in_vmem(x):
    return pltpu.with_memory_space_constraint(x, pltpu.VMEM)


def finish_kernel(keep_ref, got_ref, out_ref):
    best = jnp.maximum(keep_ref[...], got_ref[...])
    best = jnp.where(best > -100000000.0, best, jnp.float32(0.0))
    half = best.shape[1] // 2
    odd = (lax.axis_index("wide") & 1) == 1
    even_queries = jnp.where(odd, best[:, half:], best[:, :half])
    odd_queries = jnp.where(odd, best[:, :half], best[:, half:])
    low = lax.broadcasted_iota(jnp.int32, (best.shape[0], 128), 1) < 64
    for tile in range(half // 128):
        at = slice(tile * 128, (tile + 1) * 128)
        a, b = even_queries[:, at], odd_queries[:, at]
        out_ref[:, 2 * tile * 128 : (2 * tile + 1) * 128] = jnp.where(low, a, pltpu.roll(b, 64, 1))
        out_ref[:, (2 * tile + 1) * 128 : (2 * tile + 2) * 128] = jnp.where(low, pltpu.roll(a, 64, 1), b)


def finish(keep, got):
    return pl.pallas_call(
        finish_kernel,
        in_specs=[VMEM, VMEM],
        out_specs=VMEM,
        out_shape=jax.ShapeDtypeStruct(keep.shape, jnp.float32),
        compiler_params=PARAMS,
        name="finish",
    )(in_vmem(keep), in_vmem(got))


def program(hidden_states, block_owner, token_doc, token_live, proj_weight, queries):
    n = lax.axis_size("wide")
    nblocks = hidden_states.shape[0]
    if n & (n - 1) or queries.shape[0] != 64:
        raise ValueError("sizes")

    def swap(x, stride):
        return lax.ppermute(x, "wide", [(i, i ^ stride) for i in range(n)])

    strides = [1 << bit for bit in range(n.bit_length() - 1)]
    packed, meta, start = [], [], 0
    for share in PARTS:
        count = nblocks * share // sum(PARTS)
        vectors, layout = pack(hidden_states, proj_weight, token_doc, token_live, start, count)
        packed.append(vectors)
        meta.append(layout)
        start += count
    mine = queries
    for stride in reversed(strides[1:]):
        got = swap(mine, stride)
        mine = jnp.concatenate([mine, got], axis=0)
    other = swap(mine, 1)
    owner = block_owner.reshape(-1)
    keep_a, send_a = score(owner, packed, meta, mine, n)
    got_b = swap(send_a, 1)
    keep_b, send_b = score(owner, packed, meta, other, n)
    got_a = swap(send_b, 1)
    best = jnp.concatenate([jnp.maximum(keep_a, got_a), jnp.maximum(keep_b, got_b)], axis=1)
    for stride in strides[1:]:
        half = best.shape[0] // 2
        keep, got = best[:half], swap(best[half:], stride)
        if stride != strides[-1]:
            best = jnp.maximum(keep, got)
    return finish(keep, got)


def solution(mesh):
    placed = (
        P(("groups", "wide"), None, None),
        P(("groups", "wide"), None),
        P(("groups", "wide"), None),
        P(("groups", "wide"), None),
        P(),
        P(("groups", "wide"), None),
    )
    return jax.shard_map(program, mesh=mesh, in_specs=placed, out_specs=P(("groups", "wide"), None), check_vma=False)
```

profile of v0, /device:TPU:0, one launch (start us, length us, event | category | flops | bytes accessed | tf_op | source)
XLA Modules:
  0.0 49.7 jit_solution(9861176228345312555)
XLA Ops:
  0.0 0.0 copy-start.1
  0.0 4.1 %collective-permute-start = (bf16[64,128]{1,0:T(8,128)(2,1)}, bf16[64,128]{1,0:T(8,128)(2,1)S(1)}, u32[]{:S(2)}, u32[]{:S(2)}) collective-permute-start(bf16[64,128]{1,0:T(8,128)(2,1)} %param.11), channel_id=1, source_target_pairs={{0,8},{1,9},{2,10},{3,11},{4,12},{5,13},{6,14},{7,15},{8,0},{9,1},... | collective-permute-start | bytes 49160 | tf_op jit(solution)/shard_map/ppermute | solution.py:272
  4.1 0.8 %constant_dynamic-update-slice_fusion.3 = bf16[512,128]{1,0:T(8,128)(2,1)S(1)} fusion(bf16[64,128]{1,0:T(8,128)(2,1)} %param.11), kind=kLoop, calls=%fused_computation.11 | loop fusion | bytes 32768
  4.8 4.1 %pack.3 = (bf16[24,128,128]{2,1,0:T(8,128)(2,1)S(1)}, s32[24,5,8,128]{3,2,1,0:T(8,128)S(1)}) custom-call(bf16[64,64,1024]{2,1,0:T(8,128)(2,1)} %h_hbm.5, bf16[1024,128]{1,0:T(8,128)(2,1)} %w_hbm.5, s32[64,64]{1,0:T(8,128)} %doc_hbm.5, s32[64,64]{1,0:T(8,128)} %live_hbm.5), custom_call_target="tpu_custom_call" | custom-call | flops 402653184 | bytes 3145728 | tf_op jit(solution)/shard_map/pack/pallas_call | solution.py:113
  9.0 0.0 collective-permute-done
  9.0 0.0 copy-done.1
  9.0 1.6 %collective-permute-start.1 = (bf16[128,128]{1,0:T(8,128)(2,1)S(1)}, bf16[128,128]{1,0:T(8,128)(2,1)S(1)}, u32[]{:S(2)}, u32[]{:S(2)}) collective-permute-start(bf16[128,128]{1,0:T(8,128)(2,1)S(1)} %pad_maximum_fusion.2), channel_id=1, source_target_pairs={{0,4},{1,5},{2,6},{3,7},{4,0},{5,1},{6,2},{7,3},{8,12},{9,13},{10,... | collective-permute-start | bytes 98312 | tf_op jit(solution)/shard_map/ppermute | solution.py:272
  10.7 2.3 %collective-permute-done.1 = bf16[128,128]{1,0:T(8,128)(2,1)S(1)} collective-permute-done((bf16[128,128]{1,0:T(8,128)(2,1)S(1)}, bf16[128,128]{1,0:T(8,128)(2,1)S(1)}, u32[]{:S(2)}, u32[]{:S(2)}) %collective-permute-start.1) | collective-permute-done | bytes 32800 | tf_op jit(solution)/shard_map/ppermute | solution.py:272
  13.0 1.5 %collective-permute-start.2 = (bf16[256,128]{1,0:T(8,128)(2,1)S(1)}, bf16[256,128]{1,0:T(8,128)(2,1)S(1)}, u32[]{:S(2)}, u32[]{:S(2)}) collective-permute-start(bf16[256,128]{1,0:T(8,128)(2,1)S(1)} %pad_maximum_fusion.1), channel_id=1, source_target_pairs={{0,2},{1,3},{2,0},{3,1},{4,6},{5,7},{6,4},{7,5},{8,10},{9,11},{10,... | collective-permute-start | bytes 196616 | tf_op jit(solution)/shard_map/ppermute | solution.py:272
  14.5 2.7 %collective-permute-done.2 = bf16[256,128]{1,0:T(8,128)(2,1)S(1)} collective-permute-done((bf16[256,128]{1,0:T(8,128)(2,1)S(1)}, bf16[256,128]{1,0:T(8,128)(2,1)S(1)}, u32[]{:S(2)}, u32[]{:S(2)}) %collective-permute-start.2) | collective-permute-done | bytes 65568 | tf_op jit(solution)/shard_map/ppermute | solution.py:272
  17.3 0.0 copy-start
  17.3 0.1 collective-permute-start.3
  17.4 4.2 %pack.4 = (bf16[24,128,128]{2,1,0:T(8,128)(2,1)S(1)}, s32[24,5,8,128]{3,2,1,0:T(8,128)S(1)}) custom-call(bf16[64,64,1024]{2,1,0:T(8,128)(2,1)} %h_hbm.5, bf16[1024,128]{1,0:T(8,128)(2,1)} %w_hbm.5, s32[64,64]{1,0:T(8,128)} %doc_hbm.5, s32[64,64]{1,0:T(8,128)} %live_hbm.5), custom_call_target="tpu_custom_call" | custom-call | flops 402653184 | bytes 3145728 | tf_op jit(solution)/shard_map/pack/pallas_call | solution.py:113
  21.5 3.3 %pack.5 = (bf16[16,128,128]{2,1,0:T(8,128)(2,1)S(1)}, s32[16,5,8,128]{3,2,1,0:T(8,128)S(1)}) custom-call(bf16[64,64,1024]{2,1,0:T(8,128)(2,1)} %h_hbm.5, bf16[1024,128]{1,0:T(8,128)(2,1)} %w_hbm.5, s32[64,64]{1,0:T(8,128)} %doc_hbm.5, s32[64,64]{1,0:T(8,128)} %live_hbm.5), custom_call_target="tpu_custom_call" | custom-call | flops 268435456 | bytes 2097152 | tf_op jit(solution)/shard_map/pack/pallas_call | solution.py:113
  24.9 0.0 copy-done
  24.9 3.6 %shard_map.64 = (f32[64,512]{1,0:T(8,128)S(1)}, f32[64,512]{1,0:T(8,128)S(1)}) custom-call(s32[64]{0:T(128)S(1)} %bitcast.1, bf16[24,128,128]{2,1,0:T(8,128)(2,1)S(1)} %get-tuple-element.15.refs_0_, bf16[24,128,128]{2,1,0:T(8,128)(2,1)S(1)} %get-tuple-element.16.refs_1_, bf16[16,128,128]{2,1,0:T(8,128)(2,1)S(1)} %get-tuple-element.17.refs_2_, ...), custom_call_target="tpu_custom_call" | custom-call | flops 1073741824 | bytes 4194304 | tf_op jit(solution)/shard_map/pallas_call | solution.py:215
  28.5 0.6 %collective-permute-start.5 = (f32[64,512]{1,0:T(8,128)S(1)}, f32[64,512]{1,0:T(8,128)S(1)}, u32[]{:S(2)}, u32[]{:S(2)}) collective-permute-start(f32[64,512]{1,0:T(8,128)S(1)} %get-tuple-element.24), channel_id=1, source_target_pairs={{0,1},{1,0},{2,3},{3,2},{4,5},{5,4},{6,7},{7,6},{8,9},{9,8},{10,11... | collective-permute-start | bytes 393224 | tf_op jit(solution)/shard_map/ppermute | solution.py:272
  29.1 0.0 collective-permute-done.3.refs_6_
  29.1 3.6 %shard_map.65 = (f32[64,512]{1,0:T(8,128)S(1)}, f32[64,512]{1,0:T(8,128)S(1)}) custom-call(s32[64]{0:T(128)S(1)} %bitcast.2, bf16[24,128,128]{2,1,0:T(8,128)(2,1)S(1)} %get-tuple-element.15.refs_0_, bf16[24,128,128]{2,1,0:T(8,128)(2,1)S(1)} %get-tuple-element.16.refs_1_, bf16[16,128,128]{2,1,0:T(8,128)(2,1)S(1)} %get-tuple-element.17.refs_2_, ...), custom_call_target="tpu_custom_call" | custom-call | flops 1073741824 | bytes 4194304 | tf_op jit(solution)/shard_map/pallas_call | solution.py:215
  32.7 0.1 collective-permute-start.4
  32.8 0.0 collective-permute-done.5
  32.8 1.3 %collective-permute-done.4 = f32[64,512]{1,0:T(8,128)S(1)} collective-permute-done((f32[64,512]{1,0:T(8,128)S(1)}, f32[64,512]{1,0:T(8,128)S(1)}, u32[]{:S(2)}, u32[]{:S(2)}) %collective-permute-start.4) | collective-permute-done | bytes 131104 | tf_op jit(solution)/shard_map/ppermute | solution.py:272
  34.2 1.6 %collective-permute-start.6 = (f32[32,1024]{1,0:T(8,128)S(1)}, f32[32,1024]{1,0:T(8,128)S(1)}, u32[]{:S(2)}, u32[]{:S(2)}) collective-permute-start(f32[32,1024]{1,0:T(8,128)S(1)} %pad_maximum_fusion), channel_id=1, source_target_pairs={{0,2},{1,3},{2,0},{3,1},{4,6},{5,7},{6,4},{7,5},{8,10},{9,11},{10,... | collective-permute-start | bytes 393224 | tf_op jit(solution)/shard_map/ppermute | solution.py:272
  35.7 4.0 %collective-permute-done.6 = f32[32,1024]{1,0:T(8,128)S(1)} collective-permute-done((f32[32,1024]{1,0:T(8,128)S(1)}, f32[32,1024]{1,0:T(8,128)S(1)}, u32[]{:S(2)}, u32[]{:S(2)}) %collective-permute-start.6) | collective-permute-done | bytes 131104 | tf_op jit(solution)/shard_map/ppermute | solution.py:272
  39.8 1.6 %collective-permute-start.7 = (f32[16,1024]{1,0:T(8,128)S(1)}, f32[16,1024]{1,0:T(8,128)S(1)}, u32[]{:S(2)}, u32[]{:S(2)}) collective-permute-start(f32[16,1024]{1,0:T(8,128)S(1)} %slice.27), channel_id=1, source_target_pairs={{0,4},{1,5},{2,6},{3,7},{4,0},{5,1},{6,2},{7,3},{8,12},{9,13},{10,... | collective-permute-start | bytes 196616 | tf_op jit(solution)/shard_map/ppermute | solution.py:272
  41.4 2.7 %collective-permute-done.7 = f32[16,1024]{1,0:T(8,128)S(1)} collective-permute-done((f32[16,1024]{1,0:T(8,128)S(1)}, f32[16,1024]{1,0:T(8,128)S(1)}, u32[]{:S(2)}, u32[]{:S(2)}) %collective-permute-start.7) | collective-permute-done | bytes 65568 | tf_op jit(solution)/shard_map/ppermute | solution.py:272
  44.2 0.2 collective-permute-start.8
  44.3 4.7 %collective-permute-done.8.got_ref = f32[8,1024]{1,0:T(8,128)S(1)} collective-permute-done((f32[8,1024]{1,0:T(8,128)S(1)}, f32[8,1024]{1,0:T(8,128)S(1)}, u32[]{:S(2)}, u32[]{:S(2)}) %collective-permute-start.8) | collective-permute-done | bytes 32800 | tf_op jit(solution)/shard_map/ppermute | solution.py:272
  49.0 0.7 %finish.1 = f32[8,1024]{1,0:T(8,128)} custom-call(f32[8,1024]{1,0:T(8,128)S(1)} %get-tuple-element.26.keep_ref, f32[8,1024]{1,0:T(8,128)S(1)} %collective-permute-done.8.got_ref), custom_call_target="tpu_custom_call" | custom-call | tf_op jit(solution)/shard_map/finish/pallas_call | solution.py:255
  (12 shorter events, 0.1 us)
Async XLA Ops:
  0.0 9.0 %copy-start.1 = (bf16[64,128]{1,0:T(8,128)(2,1)S(1)}, bf16[64,128]{1,0:T(8,128)(2,1)}, u32[]{:S(2)}) copy-start(bf16[64,128]{1,0:T(8,128)(2,1)} %param.11) | copy-start | bytes 49156
  0.0 9.0 %collective-permute-start = (bf16[64,128]{1,0:T(8,128)(2,1)}, bf16[64,128]{1,0:T(8,128)(2,1)S(1)}, u32[]{:S(2)}, u32[]{:S(2)}) collective-permute-start(bf16[64,128]{1,0:T(8,128)(2,1)} %param.11), channel_id=1, source_target_pairs={{0,8},{1,9},{2,10},{3,11},{4,12},{5,13},{6,14},{7,15},{8,0},{9,1},... | collective-permute-start | bytes 49160 | tf_op jit(solution)/shard_map/ppermute | solution.py:272
  9.0 4.0 %collective-permute-start.1 = (bf16[128,128]{1,0:T(8,128)(2,1)S(1)}, bf16[128,128]{1,0:T(8,128)(2,1)S(1)}, u32[]{:S(2)}, u32[]{:S(2)}) collective-permute-start(bf16[128,128]{1,0:T(8,128)(2,1)S(1)} %pad_maximum_fusion.2), channel_id=1, source_target_pairs={{0,4},{1,5},{2,6},{3,7},{4,0},{5,1},{6,2},{7,3},{8,12},{9,13},{10,... | collective-permute-start | bytes 98312 | tf_op jit(solution)/shard_map/ppermute | solution.py:272
  13.0 4.3 %collective-permute-start.2 = (bf16[256,128]{1,0:T(8,128)(2,1)S(1)}, bf16[256,128]{1,0:T(8,128)(2,1)S(1)}, u32[]{:S(2)}, u32[]{:S(2)}) collective-permute-start(bf16[256,128]{1,0:T(8,128)(2,1)S(1)} %pad_maximum_fusion.1), channel_id=1, source_target_pairs={{0,2},{1,3},{2,0},{3,1},{4,6},{5,7},{6,4},{7,5},{8,10},{9,11},{10,... | collective-permute-start | bytes 196616 | tf_op jit(solution)/shard_map/ppermute | solution.py:272
  17.3 7.6 %copy-start = (s32[64,1]{0,1:T(1,128)S(1)}, s32[64,1]{0,1:T(1,128)}, u32[]{:S(2)}) copy-start(s32[64,1]{0,1:T(1,128)} %param.7) | copy-start | bytes 772
  17.3 11.8 %collective-permute-start.3 = (bf16[512,128]{1,0:T(8,128)(2,1)S(1)}, bf16[512,128]{1,0:T(8,128)(2,1)S(1)}, u32[]{:S(2)}, u32[]{:S(2)}) collective-permute-start(bf16[512,128]{1,0:T(8,128)(2,1)S(1)} %constant_dynamic-update-slice_fusion.refs_6_), channel_id=1, source_target_pairs={{0,1},{1,0},{2,3},{3,2},{4,5},{5,4},{6,7},{7,6},{8,9},{9,8},{10,11... | collective-permute-start | bytes 393224 | tf_op jit(solution)/shard_map/ppermute | solution.py:272
  28.5 4.3 %collective-permute-start.5 = (f32[64,512]{1,0:T(8,128)S(1)}, f32[64,512]{1,0:T(8,128)S(1)}, u32[]{:S(2)}, u32[]{:S(2)}) collective-permute-start(f32[64,512]{1,0:T(8,128)S(1)} %get-tuple-element.24), channel_id=1, source_target_pairs={{0,1},{1,0},{2,3},{3,2},{4,5},{5,4},{6,7},{7,6},{8,9},{9,8},{10,11... | collective-permute-start | bytes 393224 | tf_op jit(solution)/shard_map/ppermute | solution.py:272
  32.7 1.4 %collective-permute-start.4 = (f32[64,512]{1,0:T(8,128)S(1)}, f32[64,512]{1,0:T(8,128)S(1)}, u32[]{:S(2)}, u32[]{:S(2)}) collective-permute-start(f32[64,512]{1,0:T(8,128)S(1)} %get-tuple-element.22), channel_id=1, source_target_pairs={{0,1},{1,0},{2,3},{3,2},{4,5},{5,4},{6,7},{7,6},{8,9},{9,8},{10,11... | collective-permute-start | bytes 393224 | tf_op jit(solution)/shard_map/ppermute | solution.py:272
  34.2 5.6 %collective-permute-start.6 = (f32[32,1024]{1,0:T(8,128)S(1)}, f32[32,1024]{1,0:T(8,128)S(1)}, u32[]{:S(2)}, u32[]{:S(2)}) collective-permute-start(f32[32,1024]{1,0:T(8,128)S(1)} %pad_maximum_fusion), channel_id=1, source_target_pairs={{0,2},{1,3},{2,0},{3,1},{4,6},{5,7},{6,4},{7,5},{8,10},{9,11},{10,... | collective-permute-start | bytes 393224 | tf_op jit(solution)/shard_map/ppermute | solution.py:272
  39.8 4.3 %collective-permute-start.7 = (f32[16,1024]{1,0:T(8,128)S(1)}, f32[16,1024]{1,0:T(8,128)S(1)}, u32[]{:S(2)}, u32[]{:S(2)}) collective-permute-start(f32[16,1024]{1,0:T(8,128)S(1)} %slice.27), channel_id=1, source_target_pairs={{0,4},{1,5},{2,6},{3,7},{4,0},{5,1},{6,2},{7,3},{8,12},{9,13},{10,... | collective-permute-start | bytes 196616 | tf_op jit(solution)/shard_map/ppermute | solution.py:272
  44.2 4.9 %collective-permute-start.8 = (f32[8,1024]{1,0:T(8,128)S(1)}, f32[8,1024]{1,0:T(8,128)S(1)}, u32[]{:S(2)}, u32[]{:S(2)}) collective-permute-start(f32[8,1024]{1,0:T(8,128)S(1)} %get-tuple-element.25), channel_id=1, source_target_pairs={{0,8},{1,9},{2,10},{3,11},{4,12},{5,13},{6,14},{7,15},{8,0},{9,1},... | collective-permute-start | bytes 98312 | tf_op jit(solution)/shard_map/ppermute | solution.py:272
where the time goes:
time: 50 us; the launch traced here: 49.7 us
  Pallas kernels  19.6 us (39%)
  waiting for transfers between devices  17.8 us (36%)
  starting transfers between devices  11.3 us (23%)
  local copies, waits for them, and re-layouts  0.8 us (2%)
    ppermute x9, waiting for transfers between devices, swap(): return lax.ppermute(x, 'wide', [(i, i ^ stride) for i in range(n)])  17.8 us
    pallas_call x3, Pallas kernels, pack(): pl.pallas_call(functools.partial(pack_kernel, start=start), in_specs=[pl....  11.6 us
    ppermute x9, starting transfers between devices, swap(): return lax.ppermute(x, 'wide', [(i, i ^ stride) for i in range(n)])  11.3 us
    pallas_call x2, Pallas kernels, score(): pl.pallas_call(functools.partial(score_kernel, parts=len(packed), width=2...  7.23 us
  transfers between devices with their start and end apart: 9, of which 6 were waited for; matrix products, arithmetic and copies ran while one was open for 2% of the time, Pallas kernels for 38%

commit v1 on v0

v1 whole, which is shorter than its diff:
```python
import functools

import jax
import jax.numpy as jnp
from jax import lax
from jax.experimental import pallas as pl
from jax.experimental.pallas import tpu as pltpu
from jax.sharding import PartitionSpec as P


DOC_DEV = 8
CHUNK = 8
GROUP = 8
UNROLL = 24
LOW = -1000000000.0
SENT = jnp.float16
SCALE = 4096.0
NONE = -60000.0
PARTS = (2, 3, 3)

VMEM = pl.BlockSpec(memory_space=pltpu.VMEM)
PARAMS = pltpu.CompilerParams(vmem_limit_bytes=24 << 20)


def bit_reverse(value, bits):
    out = value * 0
    for bit in range(bits):
        out = out | (((value >> bit) & 1) << (bits - 1 - bit))
    return out


def place_tokens(doc, live):
    nb, bl = doc.shape
    livef = live.astype(jnp.float32)
    upto = lax.broadcasted_iota(jnp.int32, (bl, bl), 0) <= lax.broadcasted_iota(
        jnp.int32, (bl, bl), 1
    )
    counted = jnp.dot(livef, upto.astype(jnp.float32), preferred_element_type=jnp.float32)
    before = jnp.zeros((nb, bl), jnp.float32)
    extra = jnp.zeros((nb, bl), jnp.int32)
    for slot in range(DOC_DEV):
        n = jnp.sum(jnp.where(doc == slot, livef, 0.0), axis=1, keepdims=True)
        more = jnp.maximum((n.astype(jnp.int32) - 1) >> 3, 0)
        before = before + jnp.where(doc > slot, n, 0.0)
        extra = extra + jnp.where(doc > slot, more, 0)
    rank = (counted - livef - before).astype(jnp.int32)
    part, group = rank >> 3, rank & 7
    row = jnp.where(part == 0, group * 8 + doc, 64 + group * 8 + extra + part - 1)
    return jnp.where(live, row, -1), jnp.where(live, doc, -1)


def pack_blocks(project, groups, w_ref, row_ref, doc_ref, start, out_ref, meta_ref):
    bl = row_ref.shape[1]
    dim = w_ref.shape[1]
    sub = lax.broadcasted_iota(jnp.int32, (8, bl), 0)
    earlier = (
        lax.broadcasted_iota(jnp.int32, (8, 8), 0) > lax.broadcasted_iota(jnp.int32, (8, 8), 1)
    ).astype(jnp.float32)
    coming = project(0)
    for g in range(groups):
        vectors = coming
        if g + 1 < groups:
            coming = project(g + 1)
        for u in range(GROUP):
            b = g * GROUP + u
            row = row_ref[start + b : start + b + 1, :]
            tiles, counts = [], []
            for tile in range(2):
                hits = [
                    (row == sub + (64 * tile + 8 * i)).astype(jnp.float32) for i in range(CHUNK)
                ]
                count = jnp.sum(functools.reduce(jnp.add, hits), axis=1, keepdims=True)
                counts.append(count)
                tiles += hits[:1]
                tiles += [jnp.where(count > float(i), hits[i], hits[0]) for i in range(1, CHUNK)]
            pick = jnp.concatenate(tiles, axis=0).astype(jnp.bfloat16)
            out_ref[b] = jnp.dot(
                pick, vectors[u * bl : (u + 1) * bl], preferred_element_type=jnp.float32
            ).astype(jnp.bfloat16)
            doc = doc_ref[start + b : start + b + 1, :]
            n = jnp.sum((doc == sub).astype(jnp.float32), axis=1, keepdims=True)
            n = jnp.broadcast_to(n, (8, dim)).astype(jnp.int32)
            more = jnp.maximum((n - 1) >> 3, 0)
            first = jnp.dot(
                earlier, more.astype(jnp.float32), preferred_element_type=jnp.float32
            ).astype(jnp.int32)
            for tile in range(2):
                meta_ref[b, tile] = jnp.broadcast_to((counts[tile] > 0).astype(jnp.int32), (8, dim))
            for j in range(3):
                meta_ref[b, 2 + j] = jnp.where(more > j, first + j, 7)


def vectors_of(h, w):
    projected = jnp.dot(h.reshape(-1, h.shape[-1]), w, preferred_element_type=jnp.float32)
    total = jnp.sum(projected * projected, axis=1, keepdims=True)
    return (projected * lax.rsqrt(total + 1e-06)).astype(jnp.bfloat16)


def pack_first_kernel(
    h_hbm, w_hbm, doc_hbm, live_hbm, out_ref, meta_ref, next_ref, w_ref, row_ref, doc_ref, *scratch
):
    h_ref, token_ref, live_ref, sems = scratch
    nb, count = h_ref.shape[0], next_ref.shape[0]
    groups = nb // GROUP
    small = [
        pltpu.make_async_copy(doc_hbm, token_ref, sems.at[0]),
        pltpu.make_async_copy(live_hbm, live_ref, sems.at[1]),
        pltpu.make_async_copy(w_hbm, w_ref, sems.at[2]),
    ]
    large = [
        pltpu.make_async_copy(
            h_hbm.at[pl.ds(g * GROUP, GROUP)], h_ref.at[pl.ds(g * GROUP, GROUP)], sems.at[4 + g]
        )
        for g in range(groups)
    ]
    later = pltpu.make_async_copy(h_hbm.at[pl.ds(nb, count)], next_ref, sems.at[3])
    for copy in small + large + [later]:
        copy.start()
    small[0].wait()
    small[1].wait()
    row, doc = place_tokens(token_ref[...], live_ref[...] == 1)
    row_ref[...] = row
    doc_ref[...] = doc
    small[2].wait()

    def project(g):
        large[g].wait()
        return vectors_of(h_ref[g * GROUP : (g + 1) * GROUP], w_ref[...])

    pack_blocks(project, groups, w_ref, row_ref, doc_ref, 0, out_ref, meta_ref)
    later.wait()


def pack_next_kernel(h_ref, w_ref, row_ref, doc_ref, *refs, start, more):
    nb = h_ref.shape[0]
    if more:
        h_hbm, out_ref, meta_ref, next_ref, sem = refs
        later = pltpu.make_async_copy(
            h_hbm.at[pl.ds(start + nb, next_ref.shape[0])], next_ref, sem.at[0]
        )
        later.start()
    else:
        out_ref, meta_ref = refs

    def project(g):
        return vectors_of(h_ref[g * GROUP : (g + 1) * GROUP], w_ref[...])

    pack_blocks(project, nb // GROUP, w_ref, row_ref, doc_ref, start, out_ref, meta_ref)
    if more:
        later.wait()


def pack(hidden_states, proj_weight, token_doc, token_live):
    nblocks, bl, d = hidden_states.shape
    dim = proj_weight.shape[1]
    sizes = [nblocks * share // sum(PARTS) for share in PARTS]
    starts = [sum(sizes[:i]) for i in range(len(sizes))]
    hidden = in_hbm(hidden_states)

    def outputs(i):
        shapes = [
            pltpu.VMEM((sizes[i], 128, dim), jnp.bfloat16),
            pltpu.VMEM((sizes[i], 5, 8, dim), jnp.int32),
        ]
        if i + 1 < len(sizes):
            shapes.append(pltpu.VMEM((sizes[i + 1], bl, d), hidden_states.dtype))
        return shapes

    def cost(i):
        tokens = sizes[i] * bl
        return pl.CostEstimate(
            flops=2 * tokens * d * dim, bytes_accessed=2 * tokens * d, transcendentals=tokens
        )

    def first():
        shapes = outputs(0) + [
            pltpu.VMEM((d, dim), proj_weight.dtype),
            pltpu.VMEM((nblocks, bl), jnp.int32),
            pltpu.VMEM((nblocks, bl), jnp.int32),
        ]
        return pl.pallas_call(
            pack_first_kernel,
            in_specs=[pl.BlockSpec(memory_space=pltpu.HBM)] * 4,
            out_specs=[VMEM] * len(shapes),
            out_shape=shapes,
            scratch_shapes=[
                pltpu.VMEM((sizes[0], bl, d), hidden_states.dtype),
                pltpu.VMEM((nblocks, bl), jnp.int32),
                pltpu.VMEM((nblocks, bl), jnp.int32),
                pltpu.SemaphoreType.DMA((4 + sizes[0] // GROUP,)),
            ],
            cost_estimate=cost(0),
            compiler_params=PARAMS,
            name="pack_first",
        )(hidden, *(in_hbm(x) for x in (proj_weight, token_doc, token_live)))

    def following(i, fetched, weight, row, doc):
        more = i + 1 < len(sizes)
        return pl.pallas_call(
            functools.partial(pack_next_kernel, start=starts[i], more=more),
            in_specs=[VMEM] * 4 + [pl.BlockSpec(memory_space=pltpu.HBM)] * more,
            out_specs=[VMEM] * (3 if more else 2),
            out_shape=outputs(i),
            scratch_shapes=[pltpu.SemaphoreType.DMA((1,))] * more,
            cost_estimate=cost(i),
            compiler_params=PARAMS,
            name="pack_next",
        )(fetched, weight, row, doc, *[hidden] * more)

    packed, meta = [], []
    for i in range(len(sizes)):
        if i == 0:
            vectors, layout, *left, weight, row, doc = first()
        else:
            vectors, layout, *left = following(i, left[0], weight, row, doc)
        packed.append(vectors)
        meta.append(layout)
    return packed, meta


def score_kernel(owner_ref, *refs, parts, pieces, width):
    vec_refs, meta_refs = refs[:parts], refs[parts : 2 * parts]
    got_refs = refs[2 * parts : 2 * parts + pieces]
    keep_ref, send_ref, unit_ref, query_ref, table_ref = refs[2 * parts + pieces :]
    n = lax.axis_size("wide")
    bits = n.bit_length() - 1
    me = lax.axis_index("wide")
    columns = query_ref.shape[0]
    piece = columns // (n // 2)
    largest = jnp.zeros((16, query_ref.shape[1]), jnp.float32)
    j = 0
    for got_ref in got_refs:
        for k in range(got_ref.shape[0] // piece):
            chip = (me >> 1) ^ bit_reverse(j, bits - 1)
            block = got_ref[k * piece : (k + 1) * piece, :]
            query_ref[pl.ds(pl.multiple_of(chip * piece, piece), piece), :] = block
            size = jnp.abs(block.astype(jnp.float32))
            for r in range(0, piece, 16):
                largest = jnp.maximum(largest, size[r : r + 16])
            j += 1
    unit = jnp.max(jnp.max(largest, axis=1, keepdims=True), axis=0, keepdims=True)
    unit = jnp.broadcast_to(jnp.where(unit > 0.0, unit, 1.0) * (1.0 / SCALE), unit_ref.shape)
    unit_ref[...] = unit
    table_ref[...] = jnp.full(table_ref.shape, LOW, jnp.float32)
    span = min(columns, 512)

    def visit(vec_ref, meta_ref, b, offset, start):
        place = bit_reverse(owner_ref[offset + b] ^ me, bits)
        rows = pl.ds(pl.multiple_of(place * DOC_DEV, DOC_DEV), DOC_DEV)
        some = [meta_ref[b, tile] > 0 for tile in range(2)]
        index = [meta_ref[b, 2 + j] for j in range(3)]
        tokens = vec_ref[b]
        for t in range(span // width):
            at = pl.ds(start + t * width, width)
            similar = lax.dot_general(
                tokens,
                query_ref[at, :],
                (((1,), (1,)), ((), ())),
                preferred_element_type=jnp.float32,
            )
            first, rest = (
                functools.reduce(
                    jnp.maximum,
                    [similar[64 * tile + 8 * g : 64 * tile + 8 * g + 8] for g in range(CHUNK)],
                )
                for tile in range(2)
            )
            best = []
            for c in range(width // 128):
                top = jnp.where(some[0], first[:, c * 128 : (c + 1) * 128], LOW)
                further = jnp.where(some[1], rest[:, c * 128 : (c + 1) * 128], LOW)
                for j in range(3):
                    top = jnp.maximum(top, jnp.take_along_axis(further, index[j], axis=0))
                best.append(top)
            table_ref[rows, at] = jnp.maximum(table_ref[rows, at], jnp.concatenate(best, axis=1))

    def over_blocks(start):
        offset = 0
        for vec_ref, meta_ref in zip(vec_refs, meta_refs):
            nb = vec_ref.shape[0]
            step = next(s for s in (UNROLL, 16, 8, 4, 2, 1) if nb % s == 0)

            def some_blocks(i, carry, vec_ref=vec_ref, meta_ref=meta_ref, offset=offset, step=step):
                for u in range(step):
                    visit(vec_ref, meta_ref, i * step + u, offset, start)
                return carry

            lax.fori_loop(0, nb // step, some_blocks, 0)
            offset += nb

    if columns == span:
        over_blocks(0)
    else:

        def one_span(i, carry):
            over_blocks(pl.multiple_of(i * span, span))
            return carry

        lax.fori_loop(0, columns // span, one_span, 0)
    half = table_ref.shape[0] // 2
    factor = 1.0 / unit[:1, :1]
    keep_ref[...] = jnp.maximum(table_ref[:half, :] * factor, NONE)
    send_ref[...] = jnp.maximum(table_ref[half:, :] * factor, NONE)


def score(owner, packed, meta, gathered, owners):
    dim = gathered[0].shape[1]
    columns = sum(piece.shape[0] for piece in gathered)
    rows = sum(p.shape[0] * p.shape[1] for p in packed)
    half = (owners * DOC_DEV // 2, columns)
    return pl.pallas_call(
        functools.partial(score_kernel, parts=len(packed), pieces=len(gathered), width=256),
        in_specs=[pl.BlockSpec(memory_space=pltpu.SMEM)] + [VMEM] * (2 * len(packed) + len(gathered)),
        out_specs=[VMEM] * 3,
        out_shape=[
            pltpu.VMEM(half, jnp.float32),
            pltpu.VMEM(half, jnp.float32),
            pltpu.VMEM((8, 128), jnp.float32),
        ],
        scratch_shapes=[
            pltpu.VMEM((columns, dim), jnp.bfloat16),
            pltpu.VMEM((owners * DOC_DEV, columns), jnp.float32),
        ],
        cost_estimate=pl.CostEstimate(
            flops=2 * rows * dim * columns, bytes_accessed=4 * rows * dim, transcendentals=0
        ),
        compiler_params=PARAMS,
    )(owner, *packed, *meta, *(in_vmem(x) for x in gathered))


def in_hbm(x):
    return pltpu.with_memory_space_constraint(x, pltpu.HBM)


def in_vmem(x):
    return pltpu.with_memory_space_constraint(x, pltpu.VMEM)


def finish_kernel(keep_ref, got_ref, unit_a_ref, unit_b_ref, out_ref):
    best = jnp.maximum(keep_ref[...], got_ref[...])
    half = best.shape[1] // 2
    best = jnp.where(best > 0.9 * NONE, best, 0.0)
    best = jnp.concatenate(
        [best[:, :half] * unit_a_ref[:1, :1], best[:, half:] * unit_b_ref[:1, :1]], axis=1
    )
    odd = (lax.axis_index("wide") & 1) == 1
    even_queries = jnp.where(odd, best[:, half:], best[:, :half])
    odd_queries = jnp.where(odd, best[:, :half], best[:, half:])
    low = lax.broadcasted_iota(jnp.int32, (best.shape[0], 128), 1) < 64
    for tile in range(half // 128):
        at = slice(tile * 128, (tile + 1) * 128)
        a, b = even_queries[:, at], odd_queries[:, at]
        out_ref[:, 2 * tile * 128 : (2 * tile + 1) * 128] = jnp.where(low, a, pltpu.roll(b, 64, 1))
        out_ref[:, (2 * tile + 1) * 128 : (2 * tile + 2) * 128] = jnp.where(low, pltpu.roll(a, 64, 1), b)


def finish(keep, got, unit_a, unit_b):
    return pl.pallas_call(
        finish_kernel,
        in_specs=[VMEM] * 4,
        out_specs=VMEM,
        out_shape=jax.ShapeDtypeStruct(keep.shape, jnp.float32),
        compiler_params=PARAMS,
        name="finish",
    )(*(in_vmem(x) for x in (keep, got, unit_a, unit_b)))


def program(hidden_states, block_owner, token_doc, token_live, proj_weight, queries):
    n = lax.axis_size("wide")
    if n & (n - 1) or queries.shape[0] != 64:
        raise ValueError("sizes")

    def swap(x, stride):
        return lax.ppermute(x, "wide", [(i, i ^ stride) for i in range(n)])

    strides = [1 << bit for bit in range(n.bit_length() - 1)]
    packed, meta = pack(hidden_states, proj_weight, token_doc, token_live)
    pieces, mine = [queries], queries
    for stride in reversed(strides[1:]):
        pieces.append(swap(mine, stride))
        mine = lax.optimization_barrier(jnp.concatenate([mine, pieces[-1]], axis=0))
    other = swap(mine, 1)
    owner = block_owner.reshape(-1)
    keep_a, send_a, unit_a = score(owner, packed, meta, pieces, n)
    got_b = swap(send_a.astype(SENT), 1)
    keep_b, send_b, unit_b = score(owner, packed, meta, [other], n)
    got_a = swap(send_b.astype(SENT), 1)
    best = jnp.concatenate(
        [
            jnp.maximum(keep_a, got_a.astype(jnp.float32)),
            jnp.maximum(keep_b, got_b.astype(jnp.float32)),
        ],
        axis=1,
    )
    for stride in strides[1:]:
        half = best.shape[0] // 2
        keep, got = best[:half], swap(best[half:].astype(SENT), stride)
        if stride != strides[-1]:
            best = jnp.maximum(keep, got.astype(jnp.float32))
    return finish(keep, got.astype(jnp.float32), unit_a, unit_b)


def solution(mesh):
    placed = (
        P(("groups", "wide"), None, None),
        P(("groups", "wide"), None),
        P(("groups", "wide"), None),
        P(("groups", "wide"), None),
        P(),
        P(("groups", "wide"), None),
    )
    return jax.shard_map(
        program, mesh=mesh, in_specs=placed, out_specs=P(("groups", "wide"), None), check_vma=False
    )
```

time: 50 us -> 43.1 us (0.86)
  Pallas kernels: 19.6 us -> 15 us
  waiting for transfers between devices: 17.8 us -> 13.8 us
  starting transfers between devices: 11.3 us -> 13 us
  local copies, waits for them, and re-layouts: 0.8 us -> 0.01 us
  other arithmetic: 0.09 us -> 0.86 us
    pallas_call x6, Pallas kernels: 19.6 us -> 15 us  [the longest x2 5.91 us: score(): pl.pallas_call(functools.partial(score_kernel, parts=len(packed), pieces=...]
    ppermute x9, waiting for transfers between devices: 17.8 us -> 13.8 us  [swap(): return lax.ppermute(x, 'wide', [(i, i ^ stride) for i in range(n)])]
    ppermute x9, starting transfers between devices: 11.3 us -> 13 us  [swap(): return lax.ppermute(x, 'wide', [(i, i ^ stride) for i in range(n)])]
    unnamed x7 -> x4, local copies, waits for them, and re-layouts: 0.78 us -> 0.01 us
    concatenate x3, other arithmetic: 0.02 us -> 0.74 us  [program(): mine = lax.optimization_barrier(jnp.concatenate([mine, pieces[-1]], axis=0))]
  transfers between devices with their start and end apart: 9 -> 9, of which waited for: 6 -> 6; matrix products, arithmetic and copies ran while one was open for 2% -> 0% of each run, Pallas kernels for 38% -> 33%
where the time goes in v1:
time: 43.1 us; the launch traced here: 42.8 us
  Pallas kernels  15 us (35%)
  waiting for transfers between devices  13.8 us (32%)
  starting transfers between devices  13 us (30%)
  other arithmetic  0.86 us (2%)
    ppermute x9, waiting for transfers between devices, swap(): return lax.ppermute(x, 'wide', [(i, i ^ stride) for i in range(n)])  13.8 us
    ppermute x9, starting transfers between devices, swap(): return lax.ppermute(x, 'wide', [(i, i ^ stride) for i in range(n)])  13 us
    pallas_call x2, Pallas kernels, score(): pl.pallas_call(functools.partial(score_kernel, parts=len(packed), pieces=...  5.91 us
    pallas_call x2, Pallas kernels, following(): pl.pallas_call(functools.partial(pack_next_kernel, start=starts[i], more=...  5.28 us
    pallas_call x1, Pallas kernels, first(): pl.pallas_call(pack_first_kernel, in_specs=[pl.BlockSpec(memory_space=plt...  3.11 us
  transfers between devices with their start and end apart: 9, of which 6 were waited for; matrix products, arithmetic and copies ran while one was open for 0% of the time, Pallas kernels for 33%

profile of v1, /device:TPU:0, one launch (start us, length us, event | category | flops | bytes accessed | tf_op | source)
XLA Modules:
  0.0 42.8 jit_solution(7703469799164110438)
XLA Ops:
  0.0 4.1 %collective-permute-start = (bf16[64,128]{1,0:T(8,128)(2,1)}, bf16[64,128]{1,0:T(8,128)(2,1)S(1)}, u32[]{:S(2)}, u32[]{:S(2)}) collective-permute-start(bf16[64,128]{1,0:T(8,128)(2,1)} %refs_6_.1), channel_id=1, source_target_pairs={{0,8},{1,9},{2,10},{3,11},{4,12},{5,13},{6,14},{7,15},{8,0},{9,1},... | collective-permute-start | bytes 49160 | tf_op jit(solution)/shard_map/ppermute | solution.py:374
  4.1 1.9 %collective-permute-done.refs_7_ = bf16[64,128]{1,0:T(8,128)(2,1)S(1)} collective-permute-done((bf16[64,128]{1,0:T(8,128)(2,1)}, bf16[64,128]{1,0:T(8,128)(2,1)S(1)}, u32[]{:S(2)}, u32[]{:S(2)}) %collective-permute-start) | collective-permute-done | bytes 16416 | tf_op jit(solution)/shard_map/ppermute | solution.py:374
  6.0 0.7 %pad_maximum_fusion.3 = bf16[128,128]{1,0:T(8,128)(2,1)S(1)} fusion(bf16[64,128]{1,0:T(8,128)(2,1)S(1)} %collective-permute-done.refs_7_, bf16[64,128]{1,0:T(8,128)(2,1)} %refs_6_.1), kind=kLoop, calls=%fused_computation.13 | loop fusion | flops 65536 | bytes 65536 | tf_op jit(solution)/shard_map/concatenate | solution.py:381
  6.7 1.9 %collective-permute-start.1 = (bf16[128,128]{1,0:T(8,128)(2,1)S(1)}, bf16[128,128]{1,0:T(8,128)(2,1)S(1)}, u32[]{:S(2)}, u32[]{:S(2)}) collective-permute-start(bf16[128,128]{1,0:T(8,128)(2,1)S(1)} %pad_maximum_fusion.3), channel_id=1, source_target_pairs={{0,4},{1,5},{2,6},{3,7},{4,0},{5,1},{6,2},{7,3},{8,12},{9,13},{10,... | collective-permute-start | bytes 98312 | tf_op jit(solution)/shard_map/ppermute | solution.py:374
  8.6 2.0 %collective-permute-done.1.refs_8_ = bf16[128,128]{1,0:T(8,128)(2,1)S(1)} collective-permute-done((bf16[128,128]{1,0:T(8,128)(2,1)S(1)}, bf16[128,128]{1,0:T(8,128)(2,1)S(1)}, u32[]{:S(2)}, u32[]{:S(2)}) %collective-permute-start.1) | collective-permute-done | bytes 32800 | tf_op jit(solution)/shard_map/ppermute | solution.py:374
  10.6 1.9 %collective-permute-start.2 = (bf16[256,128]{1,0:T(8,128)(2,1)S(1)}, bf16[256,128]{1,0:T(8,128)(2,1)S(1)}, u32[]{:S(2)}, u32[]{:S(2)}) collective-permute-start(bf16[256,128]{1,0:T(8,128)(2,1)S(1)} %pad_maximum_fusion.2), channel_id=1, source_target_pairs={{0,2},{1,3},{2,0},{3,1},{4,6},{5,7},{6,4},{7,5},{8,10},{9,11},{10,... | collective-permute-start | bytes 196616 | tf_op jit(solution)/shard_map/ppermute | solution.py:374
  12.5 3.1 %pack_first.1 = (bf16[16,128,128]{2,1,0:T(8,128)(2,1)S(1)}, s32[16,5,8,128]{3,2,1,0:T(8,128)S(1)}, bf16[24,64,1024]{2,1,0:T(8,128)(2,1)S(1)}, bf16[1024,128]{1,0...) custom-call(bf16[64,64,1024]{2,1,0:T(8,128)(2,1)} %refs_0_.1, bf16[1024,128]{1,0:T(8,128)(2,1)} %w_hbm.1, ...), custom_call_target="tpu_custom_call" | custom-call | flops 268435456 | bytes 2097152 | tf_op jit(solution)/shard_map/pack_first/pallas_call | solution.py:181
  15.7 3.5 %pack_next.2 = (bf16[24,128,128]{2,1,0:T(8,128)(2,1)S(1)}, s32[24,5,8,128]{3,2,1,0:T(8,128)S(1)}, bf16[24,64,1024]{2,1,0:T(8,128)(2,1)S(1)}) custom-call(bf16[24,64,1024]{2,1,0:T(8,128)(2,1)S(1)} %get-tuple-element.23.h_ref, bf16[1024,128]{1,0:T(8,128)(2,1)S(1)} %get-tuple-element.24.w_ref, s32[64,64]{1,0:T(8,128)S(1)} %get-tuple-element.25.row_ref, ...), custom_call_target="tpu_custom_call" | custom-call | flops 402653184 | bytes 3145728 | tf_op jit(solution)/shard_map/pack_next/pallas_call | solution.py:199
  19.1 0.0 copy-start
  19.1 0.0 copy-start.1
  19.2 0.0 collective-permute-done.2.refs_9_
  19.2 0.1 collective-permute-start.3
  19.3 1.8 %pack_next.3 = (bf16[24,128,128]{2,1,0:T(8,128)(2,1)S(1)}, s32[24,5,8,128]{3,2,1,0:T(8,128)S(1)}) custom-call(bf16[24,64,1024]{2,1,0:T(8,128)(2,1)S(1)} %get-tuple-element.28.h_ref, bf16[1024,128]{1,0:T(8,128)(2,1)S(1)} %get-tuple-element.24.w_ref, s32[64,64]{1,0:T(8,128)S(1)} %get-tuple-element.25.row_ref, s32[64,64]{1,0:T(8,128)S(1)} %get-tuple-element.26.doc_ref), custom_call_target="tpu_custom_call" | custom-call | flops 402653184 | bytes 3145728 | tf_op jit(solution)/shard_map/pack_next/pallas_call | solution.py:199
  21.1 0.0 copy-done
  21.1 0.0 copy-done.1
  21.1 3.0 %shard_map.64 = (f32[64,512]{1,0:T(8,128)S(1)}, f32[64,512]{1,0:T(8,128)S(1)}, f32[8,128]{1,0:T(8,128)S(1)}) custom-call(s32[64]{0:T(128)S(1)} %bitcast.1, bf16[16,128,128]{2,1,0:T(8,128)(2,1)S(1)} %get-tuple-element.22.refs_0_, bf16[24,128,128]{2,1,0:T(8,128)(2,1)S(1)} %get-tuple-element.27.refs_1_, bf16[24,128,128]{2,1,0:T(8,128)(2,1)S(1)} %get-tuple-element.29.refs_2_, ...), custom_call_target="tpu_custom_call" | custom-call | flops 1073741824 | bytes 4194304 | tf_op jit(solution)/shard_map/pallas_call | solution.py:311
  24.1 0.6 %collective-permute-start.5 = (f16[64,512]{1,0:T(8,128)(2,1)S(1)}, f16[64,512]{1,0:T(8,128)(2,1)S(1)}, u32[]{:S(2)}, u32[]{:S(2)}) collective-permute-start(f16[64,512]{1,0:T(8,128)(2,1)S(1)} %convert_element_type.26), channel_id=1, source_target_pairs={{0,1},{1,0},{2,3},{3,2},{4,5},{5,4},{6,7},{7,6},{8,9},{9,8},{10,11... | collective-permute-start | bytes 196616 | tf_op jit(solution)/shard_map/ppermute | solution.py:374
  24.7 0.0 collective-permute-done.3.refs_6_
  24.7 3.0 %shard_map.65 = (f32[64,512]{1,0:T(8,128)S(1)}, f32[64,512]{1,0:T(8,128)S(1)}, f32[8,128]{1,0:T(8,128)S(1)}) custom-call(s32[64]{0:T(128)S(1)} %bitcast.2, bf16[16,128,128]{2,1,0:T(8,128)(2,1)S(1)} %get-tuple-element.22.refs_0_, bf16[24,128,128]{2,1,0:T(8,128)(2,1)S(1)} %get-tuple-element.27.refs_1_, bf16[24,128,128]{2,1,0:T(8,128)(2,1)S(1)} %get-tuple-element.29.refs_2_, ...), custom_call_target="tpu_custom_call" | custom-call | flops 1073741824 | bytes 4194304 | tf_op jit(solution)/shard_map/pallas_call | solution.py:311
  27.6 0.1 collective-permute-start.4
  27.7 0.0 collective-permute-done.5
  27.8 1.2 %collective-permute-done.4 = f16[64,512]{1,0:T(8,128)(2,1)S(1)} collective-permute-done((f16[64,512]{1,0:T(8,128)(2,1)S(1)}, f16[64,512]{1,0:T(8,128)(2,1)S(1)}, u32[]{:S(2)}, u32[]{:S(2)}) %collective-permute-start.4) | collective-permute-done | bytes 65568 | tf_op jit(solution)/shard_map/ppermute | solution.py:374
  29.0 0.2 collective-permute-start.6
  29.2 4.1 %collective-permute-done.6 = f16[32,1024]{1,0:T(8,128)(2,1)S(1)} collective-permute-done((f16[32,1024]{1,0:T(8,128)(2,1)S(1)}, f16[32,1024]{1,0:T(8,128)(2,1)S(1)}, u32[]{:S(2)}, u32[]{:S(2)}) %collective-permute-start.6) | collective-permute-done | bytes 65568 | tf_op jit(solution)/shard_map/ppermute | solution.py:374
  33.4 1.6 %collective-permute-start.7 = (f16[16,1024]{1,0:T(8,128)(2,1)S(1)}, f16[16,1024]{1,0:T(8,128)(2,1)S(1)}, u32[]{:S(2)}, u32[]{:S(2)}) collective-permute-start(f16[16,1024]{1,0:T(8,128)(2,1)S(1)} %slice_convert_fusion), channel_id=1, source_target_pairs={{0,4},{1,5},{2,6},{3,7},{4,0},{5,1},{6,2},{7,3},{8,12},{9,13},{10,... | collective-permute-start | bytes 98312 | tf_op jit(solution)/shard_map/ppermute | solution.py:374
  35.0 2.4 %collective-permute-done.7 = f16[16,1024]{1,0:T(8,128)(2,1)S(1)} collective-permute-done((f16[16,1024]{1,0:T(8,128)(2,1)S(1)}, f16[16,1024]{1,0:T(8,128)(2,1)S(1)}, u32[]{:S(2)}, u32[]{:S(2)}) %collective-permute-start.7) | collective-permute-done | bytes 32800 | tf_op jit(solution)/shard_map/ppermute | solution.py:374
  37.4 2.6 %collective-permute-start.8 = (f16[8,1024]{1,0:T(8,128)(2,1)S(1)}, f16[8,1024]{1,0:T(8,128)(2,1)S(1)}, u32[]{:S(2)}, u32[]{:S(2)}) collective-permute-start(f16[8,1024]{1,0:T(8,128)(2,1)S(1)} %get-tuple-element.39), channel_id=1, source_target_pairs={{0,8},{1,9},{2,10},{3,11},{4,12},{5,13},{6,14},{7,15},{8,0},{9,1},... | collective-permute-start | bytes 49160 | tf_op jit(solution)/shard_map/ppermute | solution.py:374
  40.0 2.1 %collective-permute-done.8 = f16[8,1024]{1,0:T(8,128)(2,1)S(1)} collective-permute-done((f16[8,1024]{1,0:T(8,128)(2,1)S(1)}, f16[8,1024]{1,0:T(8,128)(2,1)S(1)}, u32[]{:S(2)}, u32[]{:S(2)}) %collective-permute-start.8) | collective-permute-done | bytes 16416 | tf_op jit(solution)/shard_map/ppermute | solution.py:374
  42.1 0.7 %finish.1 = f32[8,1024]{1,0:T(8,128)} custom-call(f32[8,1024]{1,0:T(8,128)S(1)} %get-tuple-element.40.keep_ref, f32[8,1024]{1,0:T(8,128)S(1)} %convert_element_type.30.got_ref, f32[8,128]{1,0:T(8,128)S(1)} %get-tuple-element.37.unit_a_ref, f32[8,128]{1,0:T(8,128)S(1)} %get-tuple-element.38.unit_b_ref), custom_call_target="tpu_custom_call" | custom-call | tf_op jit(solution)/shard_map/finish/pallas_call | solution.py:358
  (12 shorter events, 0.1 us)
Async XLA Ops:
  0.0 6.0 %collective-permute-start = (bf16[64,128]{1,0:T(8,128)(2,1)}, bf16[64,128]{1,0:T(8,128)(2,1)S(1)}, u32[]{:S(2)}, u32[]{:S(2)}) collective-permute-start(bf16[64,128]{1,0:T(8,128)(2,1)} %refs_6_.1), channel_id=1, source_target_pairs={{0,8},{1,9},{2,10},{3,11},{4,12},{5,13},{6,14},{7,15},{8,0},{9,1},... | collective-permute-start | bytes 49160 | tf_op jit(solution)/shard_map/ppermute | solution.py:374
  6.7 3.9 %collective-permute-start.1 = (bf16[128,128]{1,0:T(8,128)(2,1)S(1)}, bf16[128,128]{1,0:T(8,128)(2,1)S(1)}, u32[]{:S(2)}, u32[]{:S(2)}) collective-permute-start(bf16[128,128]{1,0:T(8,128)(2,1)S(1)} %pad_maximum_fusion.3), channel_id=1, source_target_pairs={{0,4},{1,5},{2,6},{3,7},{4,0},{5,1},{6,2},{7,3},{8,12},{9,13},{10,... | collective-permute-start | bytes 98312 | tf_op jit(solution)/shard_map/ppermute | solution.py:374
  10.6 8.5 %collective-permute-start.2 = (bf16[256,128]{1,0:T(8,128)(2,1)S(1)}, bf16[256,128]{1,0:T(8,128)(2,1)S(1)}, u32[]{:S(2)}, u32[]{:S(2)}) collective-permute-start(bf16[256,128]{1,0:T(8,128)(2,1)S(1)} %pad_maximum_fusion.2), channel_id=1, source_target_pairs={{0,2},{1,3},{2,0},{3,1},{4,6},{5,7},{6,4},{7,5},{8,10},{9,11},{10,... | collective-permute-start | bytes 196616 | tf_op jit(solution)/shard_map/ppermute | solution.py:374
  19.1 2.0 %copy-start = (bf16[64,128]{1,0:T(8,128)(2,1)S(1)}, bf16[64,128]{1,0:T(8,128)(2,1)}, u32[]{:S(2)}) copy-start(bf16[64,128]{1,0:T(8,128)(2,1)} %refs_6_.1) | copy-start | bytes 49156
  19.1 2.0 %copy-start.1 = (s32[64,1]{0,1:T(1,128)S(1)}, s32[64,1]{0,1:T(1,128)}, u32[]{:S(2)}) copy-start(s32[64,1]{0,1:T(1,128)} %param.7) | copy-start | bytes 772
  19.2 5.5 %collective-permute-start.3 = (bf16[512,128]{1,0:T(8,128)(2,1)S(1)}, bf16[512,128]{1,0:T(8,128)(2,1)S(1)}, u32[]{:S(2)}, u32[]{:S(2)}) collective-permute-start(bf16[512,128]{1,0:T(8,128)(2,1)S(1)} %pad_maximum_fusion.1), channel_id=1, source_target_pairs={{0,1},{1,0},{2,3},{3,2},{4,5},{5,4},{6,7},{7,6},{8,9},{9,8},{10,11... | collective-permute-start | bytes 393224 | tf_op jit(solution)/shard_map/ppermute | solution.py:374
  24.1 3.6 %collective-permute-start.5 = (f16[64,512]{1,0:T(8,128)(2,1)S(1)}, f16[64,512]{1,0:T(8,128)(2,1)S(1)}, u32[]{:S(2)}, u32[]{:S(2)}) collective-permute-start(f16[64,512]{1,0:T(8,128)(2,1)S(1)} %convert_element_type.26), channel_id=1, source_target_pairs={{0,1},{1,0},{2,3},{3,2},{4,5},{5,4},{6,7},{7,6},{8,9},{9,8},{10,11... | collective-permute-start | bytes 196616 | tf_op jit(solution)/shard_map/ppermute | solution.py:374
  27.6 1.3 %collective-permute-start.4 = (f16[64,512]{1,0:T(8,128)(2,1)S(1)}, f16[64,512]{1,0:T(8,128)(2,1)S(1)}, u32[]{:S(2)}, u32[]{:S(2)}) collective-permute-start(f16[64,512]{1,0:T(8,128)(2,1)S(1)} %convert_element_type.24), channel_id=1, source_target_pairs={{0,1},{1,0},{2,3},{3,2},{4,5},{5,4},{6,7},{7,6},{8,9},{9,8},{10,11... | collective-permute-start | bytes 196616 | tf_op jit(solution)/shard_map/ppermute | solution.py:374
  29.0 4.3 %collective-permute-start.6 = (f16[32,1024]{1,0:T(8,128)(2,1)S(1)}, f16[32,1024]{1,0:T(8,128)(2,1)S(1)}, u32[]{:S(2)}, u32[]{:S(2)}) collective-permute-start(f16[32,1024]{1,0:T(8,128)(2,1)S(1)} %fusion.2), channel_id=1, source_target_pairs={{0,2},{1,3},{2,0},{3,1},{4,6},{5,7},{6,4},{7,5},{8,10},{9,11},{10,... | collective-permute-start | bytes 196616 | tf_op jit(solution)/shard_map/ppermute | solution.py:374
  33.4 4.0 %collective-permute-start.7 = (f16[16,1024]{1,0:T(8,128)(2,1)S(1)}, f16[16,1024]{1,0:T(8,128)(2,1)S(1)}, u32[]{:S(2)}, u32[]{:S(2)}) collective-permute-start(f16[16,1024]{1,0:T(8,128)(2,1)S(1)} %slice_convert_fusion), channel_id=1, source_target_pairs={{0,4},{1,5},{2,6},{3,7},{4,0},{5,1},{6,2},{7,3},{8,12},{9,13},{10,... | collective-permute-start | bytes 98312 | tf_op jit(solution)/shard_map/ppermute | solution.py:374
  37.4 4.7 %collective-permute-start.8 = (f16[8,1024]{1,0:T(8,128)(2,1)S(1)}, f16[8,1024]{1,0:T(8,128)(2,1)S(1)}, u32[]{:S(2)}, u32[]{:S(2)}) collective-permute-start(f16[8,1024]{1,0:T(8,128)(2,1)S(1)} %get-tuple-element.39), channel_id=1, source_target_pairs={{0,8},{1,9},{2,10},{3,11},{4,12},{5,13},{6,14},{7,15},{8,0},{9,1},... | collective-permute-start | bytes 49160 | tf_op jit(solution)/shard_map/ppermute | solution.py:374

commit v2 on v1

--- a/solution.py
+++ b/solution.py
@@ -16,7 +16,7 @@
 SENT = jnp.float16
 SCALE = 4096.0
 NONE = -60000.0
-PARTS = (2, 3, 3)
+PARTS = (1, 3, 4)
 
 VMEM = pl.BlockSpec(memory_space=pltpu.VMEM)
 PARAMS = pltpu.CompilerParams(vmem_limit_bytes=24 << 20)
@@ -27,6 +27,21 @@
     for bit in range(bits):
         out = out | (((value >> bit) & 1) << (bits - 1 - bit))
     return out
+
+
+def parity(value, bits):
+    out = value * 0
+    for bit in range(bits):
+        out = out ^ ((value >> bit) & 1)
+    return out
+
+
+def once(body):
+    def run(i, carry):
+        body()
+        return carry
+
+    lax.fori_loop(0, 1 + (lax.axis_index("wide") >> 20), run, 0)
 
 
 def place_tokens(doc, live):
@@ -122,12 +137,13 @@
     row_ref[...] = row
     doc_ref[...] = doc
     small[2].wait()
+    for copy in large:
+        copy.wait()
 
     def project(g):
-        large[g].wait()
         return vectors_of(h_ref[g * GROUP : (g + 1) * GROUP], w_ref[...])
 
-    pack_blocks(project, groups, w_ref, row_ref, doc_ref, 0, out_ref, meta_ref)
+    once(lambda: pack_blocks(project, groups, w_ref, row_ref, doc_ref, 0, out_ref, meta_ref))
     later.wait()
 
 
@@ -145,7 +161,8 @@
     def project(g):
         return vectors_of(h_ref[g * GROUP : (g + 1) * GROUP], w_ref[...])
 
-    pack_blocks(project, nb // GROUP, w_ref, row_ref, doc_ref, start, out_ref, meta_ref)
+    groups = nb // GROUP
+    once(lambda: pack_blocks(project, groups, w_ref, row_ref, doc_ref, start, out_ref, meta_ref))
     if more:
         later.wait()
 
@@ -245,7 +262,8 @@
     span = min(columns, 512)
 
     def visit(vec_ref, meta_ref, b, offset, start):
-        place = bit_reverse(owner_ref[offset + b] ^ me, bits)
+        apart = owner_ref[offset + b] ^ me
+        place = (parity(apart, bits) << (bits - 1)) | bit_reverse(apart >> 1, bits - 1)
         rows = pl.ds(pl.multiple_of(place * DOC_DEV, DOC_DEV), DOC_DEV)
         some = [meta_ref[b, tile] > 0 for tile in range(2)]
         index = [meta_ref[b, 2 + j] for j in range(3)]
@@ -343,15 +361,21 @@
     best = jnp.concatenate(
         [best[:, :half] * unit_a_ref[:1, :1], best[:, half:] * unit_b_ref[:1, :1]], axis=1
     )
-    odd = (lax.axis_index("wide") & 1) == 1
+    bits = lax.axis_size("wide").bit_length() - 1
+    odd = parity(lax.axis_index("wide"), bits) == 1
     even_queries = jnp.where(odd, best[:, half:], best[:, :half])
     odd_queries = jnp.where(odd, best[:, :half], best[:, half:])
     low = lax.broadcasted_iota(jnp.int32, (best.shape[0], 128), 1) < 64
-    for tile in range(half // 128):
-        at = slice(tile * 128, (tile + 1) * 128)
+    for chip in range(half // 64):
+        at = slice(chip // 2 * 128, chip // 2 * 128 + 128)
         a, b = even_queries[:, at], odd_queries[:, at]
-        out_ref[:, 2 * tile * 128 : (2 * tile + 1) * 128] = jnp.where(low, a, pltpu.roll(b, 64, 1))
-        out_ref[:, (2 * tile + 1) * 128 : (2 * tile + 2) * 128] = jnp.where(low, pltpu.roll(a, 64, 1), b)
+        if parity(chip, bits):
+            a, b = b, a
+        if chip % 2:
+            a = pltpu.roll(a, 64, 1)
+        else:
+            b = pltpu.roll(b, 64, 1)
+        out_ref[:, chip * 128 : (chip + 1) * 128] = jnp.where(low, a, b)
 
 
 def finish(keep, got, unit_a, unit_b):
@@ -373,7 +397,7 @@
     def swap(x, stride):
         return lax.ppermute(x, "wide", [(i, i ^ stride) for i in range(n)])
 
-    strides = [1 << bit for bit in range(n.bit_length() - 1)]
+    strides = [1] + [(1 << bit) | 1 for bit in range(1, n.bit_length() - 1)]
     packed, meta = pack(hidden_states, proj_weight, token_doc, token_live)
     pieces, mine = [queries], queries
     for stride in reversed(strides[1:]):

time: 43.1 us -> 39.1 us (0.907)
  waiting for transfers between devices: 13.8 us -> 11.1 us
  Pallas kernels: 15 us -> 13.9 us
    ppermute x9, waiting for transfers between devices: 13.8 us -> 11.1 us  [swap(): return lax.ppermute(x, 'wide', [(i, i ^ stride) for i in range(n)])]
    pallas_call x2, Pallas kernels: 5.28 us -> 4.18 us  [following(): pl.pallas_call(functools.partial(pack_next_kernel, start=starts[i], more=...]
    pallas_call x2, Pallas kernels: 5.91 us -> 6.65 us  [score(): pl.pallas_call(functools.partial(score_kernel, parts=len(packed), pieces=...]
    pallas_call x1, Pallas kernels: 3.11 us -> 2.37 us  [first(): pl.pallas_call(pack_first_kernel, in_specs=[pl.BlockSpec(memory_space=plt...]
  transfers between devices with their start and end apart: 9 -> 9, of which waited for: 6 -> 6; matrix products, arithmetic and copies ran while one was open for 0% -> 0% of each run, Pallas kernels for 33% -> 34%
where the time goes in v2:
time: 39.1 us; the launch traced here: 38.8 us
  Pallas kernels  13.9 us (36%)
  starting transfers between devices  12.7 us (32%)
  waiting for transfers between devices  11.1 us (28%)
  other arithmetic  0.86 us (2%)
    ppermute x9, starting transfers between devices, swap(): return lax.ppermute(x, 'wide', [(i, i ^ stride) for i in range(n)])  12.7 us
    ppermute x9, waiting for transfers between devices, swap(): return lax.ppermute(x, 'wide', [(i, i ^ stride) for i in range(n)])  11.1 us
    pallas_call x2, Pallas kernels, score(): pl.pallas_call(functools.partial(score_kernel, parts=len(packed), pieces=...  6.65 us
    pallas_call x2, Pallas kernels, following(): pl.pallas_call(functools.partial(pack_next_kernel, start=starts[i], more=...  4.18 us
    pallas_call x1, Pallas kernels, first(): pl.pallas_call(pack_first_kernel, in_specs=[pl.BlockSpec(memory_space=plt...  2.37 us
  transfers between devices with their start and end apart: 9, of which 6 were waited for; matrix products, arithmetic and copies ran while one was open for 0% of the time, Pallas kernels for 34%

profile of v2, /device:TPU:0, one launch (start us, length us, event | category | flops | bytes accessed | tf_op | source)
XLA Modules:
  0.0 38.8 jit_solution(3547421159505486693)
XLA Ops:
  0.0 3.5 %collective-permute-start = (bf16[64,128]{1,0:T(8,128)(2,1)}, bf16[64,128]{1,0:T(8,128)(2,1)S(1)}, u32[]{:S(2)}, u32[]{:S(2)}) collective-permute-start(bf16[64,128]{1,0:T(8,128)(2,1)} %refs_6_.1), channel_id=1, source_target_pairs={{0,9},{1,8},{2,11},{3,10},{4,13},{5,12},{6,15},{7,14},{8,1},{9,0},... | collective-permute-start | bytes 49160 | tf_op jit(solution)/shard_map/ppermute | solution.py:398
  3.5 1.7 %collective-permute-done.refs_7_ = bf16[64,128]{1,0:T(8,128)(2,1)S(1)} collective-permute-done((bf16[64,128]{1,0:T(8,128)(2,1)}, bf16[64,128]{1,0:T(8,128)(2,1)S(1)}, u32[]{:S(2)}, u32[]{:S(2)}) %collective-permute-start) | collective-permute-done | bytes 16416 | tf_op jit(solution)/shard_map/ppermute | solution.py:398
  5.2 0.7 %pad_maximum_fusion.3 = bf16[128,128]{1,0:T(8,128)(2,1)S(1)} fusion(bf16[64,128]{1,0:T(8,128)(2,1)S(1)} %collective-permute-done.refs_7_, bf16[64,128]{1,0:T(8,128)(2,1)} %refs_6_.1), kind=kLoop, calls=%fused_computation.13 | loop fusion | flops 65536 | bytes 65536 | tf_op jit(solution)/shard_map/concatenate | solution.py:405
  5.9 1.9 %collective-permute-start.1 = (bf16[128,128]{1,0:T(8,128)(2,1)S(1)}, bf16[128,128]{1,0:T(8,128)(2,1)S(1)}, u32[]{:S(2)}, u32[]{:S(2)}) collective-permute-start(bf16[128,128]{1,0:T(8,128)(2,1)S(1)} %pad_maximum_fusion.3), channel_id=1, source_target_pairs={{0,5},{1,4},{2,7},{3,6},{4,1},{5,0},{6,3},{7,2},{8,13},{9,12},{10,... | collective-permute-start | bytes 98312 | tf_op jit(solution)/shard_map/ppermute | solution.py:398
  7.8 1.6 %collective-permute-done.1.refs_8_ = bf16[128,128]{1,0:T(8,128)(2,1)S(1)} collective-permute-done((bf16[128,128]{1,0:T(8,128)(2,1)S(1)}, bf16[128,128]{1,0:T(8,128)(2,1)S(1)}, u32[]{:S(2)}, u32[]{:S(2)}) %collective-permute-start.1) | collective-permute-done | bytes 32800 | tf_op jit(solution)/shard_map/ppermute | solution.py:398
  9.4 1.7 %collective-permute-start.2 = (bf16[256,128]{1,0:T(8,128)(2,1)S(1)}, bf16[256,128]{1,0:T(8,128)(2,1)S(1)}, u32[]{:S(2)}, u32[]{:S(2)}) collective-permute-start(bf16[256,128]{1,0:T(8,128)(2,1)S(1)} %pad_maximum_fusion.2), channel_id=1, source_target_pairs={{0,3},{1,2},{2,1},{3,0},{4,7},{5,6},{6,5},{7,4},{8,11},{9,10},{10,... | collective-permute-start | bytes 196616 | tf_op jit(solution)/shard_map/ppermute | solution.py:398
  11.1 2.4 %pack_first.1 = (bf16[8,128,128]{2,1,0:T(8,128)(2,1)S(1)}, s32[8,5,8,128]{3,2,1,0:T(8,128)S(1)}, bf16[24,64,1024]{2,1,0:T(8,128)(2,1)S(1)}, bf16[1024,128]{1,0:T...) custom-call(bf16[64,64,1024]{2,1,0:T(8,128)(2,1)} %refs_0_.1, bf16[1024,128]{1,0:T(8,128)(2,1)} %w_hbm.1, ...), custom_call_target="tpu_custom_call" | custom-call | flops 134217728 | bytes 1048576 | tf_op jit(solution)/shard_map/pack_first/pallas_call | solution.py:198
  13.5 2.2 %pack_next.2 = (bf16[24,128,128]{2,1,0:T(8,128)(2,1)S(1)}, s32[24,5,8,128]{3,2,1,0:T(8,128)S(1)}, bf16[32,64,1024]{2,1,0:T(8,128)(2,1)S(1)}) custom-call(bf16[24,64,1024]{2,1,0:T(8,128)(2,1)S(1)} %get-tuple-element.23.h_ref, bf16[1024,128]{1,0:T(8,128)(2,1)S(1)} %get-tuple-element.24.w_ref, s32[64,64]{1,0:T(8,128)S(1)} %get-tuple-element.25.row_ref, ...), custom_call_target="tpu_custom_call" | custom-call | flops 402653184 | bytes 3145728 | tf_op jit(solution)/shard_map/pack_next/pallas_call | solution.py:216
  15.7 0.0 copy-start
  15.7 0.0 copy-start.1
  15.7 0.0 collective-permute-done.2.refs_9_
  15.8 0.5 %collective-permute-start.3 = (bf16[512,128]{1,0:T(8,128)(2,1)S(1)}, bf16[512,128]{1,0:T(8,128)(2,1)S(1)}, u32[]{:S(2)}, u32[]{:S(2)}) collective-permute-start(bf16[512,128]{1,0:T(8,128)(2,1)S(1)} %pad_maximum_fusion.1), channel_id=1, source_target_pairs={{0,1},{1,0},{2,3},{3,2},{4,5},{5,4},{6,7},{7,6},{8,9},{9,8},{10,11... | collective-permute-start | bytes 393224 | tf_op jit(solution)/shard_map/ppermute | solution.py:398
  16.2 2.0 %pack_next.3 = (bf16[32,128,128]{2,1,0:T(8,128)(2,1)S(1)}, s32[32,5,8,128]{3,2,1,0:T(8,128)S(1)}) custom-call(bf16[32,64,1024]{2,1,0:T(8,128)(2,1)S(1)} %get-tuple-element.28.h_ref, bf16[1024,128]{1,0:T(8,128)(2,1)S(1)} %get-tuple-element.24.w_ref, s32[64,64]{1,0:T(8,128)S(1)} %get-tuple-element.25.row_ref, s32[64,64]{1,0:T(8,128)S(1)} %get-tuple-element.26.doc_ref), custom_call_target="tpu_custom_call" | custom-call | flops 536870912 | bytes 4194304 | tf_op jit(solution)/shard_map/pack_next/pallas_call | solution.py:216
  18.2 0.0 copy-done
  18.2 0.0 copy-done.1
  18.2 3.3 %shard_map.64 = (f32[64,512]{1,0:T(8,128)S(1)}, f32[64,512]{1,0:T(8,128)S(1)}, f32[8,128]{1,0:T(8,128)S(1)}) custom-call(s32[64]{0:T(128)S(1)} %bitcast.1, bf16[8,128,128]{2,1,0:T(8,128)(2,1)S(1)} %get-tuple-element.22.refs_0_, bf16[24,128,128]{2,1,0:T(8,128)(2,1)S(1)} %get-tuple-element.27.refs_1_, bf16[32,128,128]{2,1,0:T(8,128)(2,1)S(1)} %get-tuple-element.29.refs_2_, ...), custom_call_target="tpu_custom_call" | custom-call | flops 1073741824 | bytes 4194304 | tf_op jit(solution)/shard_map/pallas_call | solution.py:329
  21.6 0.2 collective-permute-start.5
  21.8 0.0 collective-permute-done.3.refs_6_
  21.8 3.3 %shard_map.65 = (f32[64,512]{1,0:T(8,128)S(1)}, f32[64,512]{1,0:T(8,128)S(1)}, f32[8,128]{1,0:T(8,128)S(1)}) custom-call(s32[64]{0:T(128)S(1)} %bitcast.2, bf16[8,128,128]{2,1,0:T(8,128)(2,1)S(1)} %get-tuple-element.22.refs_0_, bf16[24,128,128]{2,1,0:T(8,128)(2,1)S(1)} %get-tuple-element.27.refs_1_, bf16[32,128,128]{2,1,0:T(8,128)(2,1)S(1)} %get-tuple-element.29.refs_2_, ...), custom_call_target="tpu_custom_call" | custom-call | flops 1073741824 | bytes 4194304 | tf_op jit(solution)/shard_map/pallas_call | solution.py:329
  25.1 0.5 %collective-permute-start.4 = (f16[64,512]{1,0:T(8,128)(2,1)S(1)}, f16[64,512]{1,0:T(8,128)(2,1)S(1)}, u32[]{:S(2)}, u32[]{:S(2)}) collective-permute-start(f16[64,512]{1,0:T(8,128)(2,1)S(1)} %convert_element_type.24), channel_id=1, source_target_pairs={{0,1},{1,0},{2,3},{3,2},{4,5},{5,4},{6,7},{7,6},{8,9},{9,8},{10,11... | collective-permute-start | bytes 196616 | tf_op jit(solution)/shard_map/ppermute | solution.py:398
  25.6 0.0 collective-permute-done.5
  25.6 0.9 %collective-permute-done.4 = f16[64,512]{1,0:T(8,128)(2,1)S(1)} collective-permute-done((f16[64,512]{1,0:T(8,128)(2,1)S(1)}, f16[64,512]{1,0:T(8,128)(2,1)S(1)}, u32[]{:S(2)}, u32[]{:S(2)}) %collective-permute-start.4) | collective-permute-done | bytes 65568 | tf_op jit(solution)/shard_map/ppermute | solution.py:398
  26.5 0.2 collective-permute-start.6
  26.7 3.7 %collective-permute-done.6 = f16[32,1024]{1,0:T(8,128)(2,1)S(1)} collective-permute-done((f16[32,1024]{1,0:T(8,128)(2,1)S(1)}, f16[32,1024]{1,0:T(8,128)(2,1)S(1)}, u32[]{:S(2)}, u32[]{:S(2)}) %collective-permute-start.6) | collective-permute-done | bytes 65568 | tf_op jit(solution)/shard_map/ppermute | solution.py:398
  30.5 1.6 %collective-permute-start.7 = (f16[16,1024]{1,0:T(8,128)(2,1)S(1)}, f16[16,1024]{1,0:T(8,128)(2,1)S(1)}, u32[]{:S(2)}, u32[]{:S(2)}) collective-permute-start(f16[16,1024]{1,0:T(8,128)(2,1)S(1)} %slice_convert_fusion), channel_id=1, source_target_pairs={{0,5},{1,4},{2,7},{3,6},{4,1},{5,0},{6,3},{7,2},{8,13},{9,12},{10,... | collective-permute-start | bytes 98312 | tf_op jit(solution)/shard_map/ppermute | solution.py:398
  32.1 1.8 %collective-permute-done.7 = f16[16,1024]{1,0:T(8,128)(2,1)S(1)} collective-permute-done((f16[16,1024]{1,0:T(8,128)(2,1)S(1)}, f16[16,1024]{1,0:T(8,128)(2,1)S(1)}, u32[]{:S(2)}, u32[]{:S(2)}) %collective-permute-start.7) | collective-permute-done | bytes 32800 | tf_op jit(solution)/shard_map/ppermute | solution.py:398
  33.9 2.7 %collective-permute-start.8 = (f16[8,1024]{1,0:T(8,128)(2,1)S(1)}, f16[8,1024]{1,0:T(8,128)(2,1)S(1)}, u32[]{:S(2)}, u32[]{:S(2)}) collective-permute-start(f16[8,1024]{1,0:T(8,128)(2,1)S(1)} %get-tuple-element.39), channel_id=1, source_target_pairs={{0,9},{1,8},{2,11},{3,10},{4,13},{5,12},{6,15},{7,14},{8,1},{9,0},... | collective-permute-start | bytes 49160 | tf_op jit(solution)/shard_map/ppermute | solution.py:398
  36.7 1.4 %collective-permute-done.8 = f16[8,1024]{1,0:T(8,128)(2,1)S(1)} collective-permute-done((f16[8,1024]{1,0:T(8,128)(2,1)S(1)}, f16[8,1024]{1,0:T(8,128)(2,1)S(1)}, u32[]{:S(2)}, u32[]{:S(2)}) %collective-permute-start.8) | collective-permute-done | bytes 16416 | tf_op jit(solution)/shard_map/ppermute | solution.py:398
  38.1 0.7 %finish.1 = f32[8,1024]{1,0:T(8,128)} custom-call(f32[8,1024]{1,0:T(8,128)S(1)} %get-tuple-element.40.keep_ref, f32[8,1024]{1,0:T(8,128)S(1)} %convert_element_type.30.got_ref, f32[8,128]{1,0:T(8,128)S(1)} %get-tuple-element.37.unit_a_ref, f32[8,128]{1,0:T(8,128)S(1)} %get-tuple-element.38.unit_b_ref), custom_call_target="tpu_custom_call" | custom-call | tf_op jit(solution)/shard_map/finish/pallas_call | solution.py:382
  (12 shorter events, 0.1 us)
Async XLA Ops:
  0.0 5.2 %collective-permute-start = (bf16[64,128]{1,0:T(8,128)(2,1)}, bf16[64,128]{1,0:T(8,128)(2,1)S(1)}, u32[]{:S(2)}, u32[]{:S(2)}) collective-permute-start(bf16[64,128]{1,0:T(8,128)(2,1)} %refs_6_.1), channel_id=1, source_target_pairs={{0,9},{1,8},{2,11},{3,10},{4,13},{5,12},{6,15},{7,14},{8,1},{9,0},... | collective-permute-start | bytes 49160 | tf_op jit(solution)/shard_map/ppermute | solution.py:398
  5.9 3.5 %collective-permute-start.1 = (bf16[128,128]{1,0:T(8,128)(2,1)S(1)}, bf16[128,128]{1,0:T(8,128)(2,1)S(1)}, u32[]{:S(2)}, u32[]{:S(2)}) collective-permute-start(bf16[128,128]{1,0:T(8,128)(2,1)S(1)} %pad_maximum_fusion.3), channel_id=1, source_target_pairs={{0,5},{1,4},{2,7},{3,6},{4,1},{5,0},{6,3},{7,2},{8,13},{9,12},{10,... | collective-permute-start | bytes 98312 | tf_op jit(solution)/shard_map/ppermute | solution.py:398
  9.4 6.4 %collective-permute-start.2 = (bf16[256,128]{1,0:T(8,128)(2,1)S(1)}, bf16[256,128]{1,0:T(8,128)(2,1)S(1)}, u32[]{:S(2)}, u32[]{:S(2)}) collective-permute-start(bf16[256,128]{1,0:T(8,128)(2,1)S(1)} %pad_maximum_fusion.2), channel_id=1, source_target_pairs={{0,3},{1,2},{2,1},{3,0},{4,7},{5,6},{6,5},{7,4},{8,11},{9,10},{10,... | collective-permute-start | bytes 196616 | tf_op jit(solution)/shard_map/ppermute | solution.py:398
  15.7 2.5 %copy-start = (bf16[64,128]{1,0:T(8,128)(2,1)S(1)}, bf16[64,128]{1,0:T(8,128)(2,1)}, u32[]{:S(2)}) copy-start(bf16[64,128]{1,0:T(8,128)(2,1)} %refs_6_.1) | copy-start | bytes 49156
  15.7 2.5 %copy-start.1 = (s32[64,1]{0,1:T(1,128)S(1)}, s32[64,1]{0,1:T(1,128)}, u32[]{:S(2)}) copy-start(s32[64,1]{0,1:T(1,128)} %param.7) | copy-start | bytes 772
  15.8 6.0 %collective-permute-start.3 = (bf16[512,128]{1,0:T(8,128)(2,1)S(1)}, bf16[512,128]{1,0:T(8,128)(2,1)S(1)}, u32[]{:S(2)}, u32[]{:S(2)}) collective-permute-start(bf16[512,128]{1,0:T(8,128)(2,1)S(1)} %pad_maximum_fusion.1), channel_id=1, source_target_pairs={{0,1},{1,0},{2,3},{3,2},{4,5},{5,4},{6,7},{7,6},{8,9},{9,8},{10,11... | collective-permute-start | bytes 393224 | tf_op jit(solution)/shard_map/ppermute | solution.py:398
  21.6 4.0 %collective-permute-start.5 = (f16[64,512]{1,0:T(8,128)(2,1)S(1)}, f16[64,512]{1,0:T(8,128)(2,1)S(1)}, u32[]{:S(2)}, u32[]{:S(2)}) collective-permute-start(f16[64,512]{1,0:T(8,128)(2,1)S(1)} %convert_element_type.26), channel_id=1, source_target_pairs={{0,1},{1,0},{2,3},{3,2},{4,5},{5,4},{6,7},{7,6},{8,9},{9,8},{10,11... | collective-permute-start | bytes 196616 | tf_op jit(solution)/shard_map/ppermute | solution.py:398
  25.1 1.4 %collective-permute-start.4 = (f16[64,512]{1,0:T(8,128)(2,1)S(1)}, f16[64,512]{1,0:T(8,128)(2,1)S(1)}, u32[]{:S(2)}, u32[]{:S(2)}) collective-permute-start(f16[64,512]{1,0:T(8,128)(2,1)S(1)} %convert_element_type.24), channel_id=1, source_target_pairs={{0,1},{1,0},{2,3},{3,2},{4,5},{5,4},{6,7},{7,6},{8,9},{9,8},{10,11... | collective-permute-start | bytes 196616 | tf_op jit(solution)/shard_map/ppermute | solution.py:398
  26.5 3.9 %collective-permute-start.6 = (f16[32,1024]{1,0:T(8,128)(2,1)S(1)}, f16[32,1024]{1,0:T(8,128)(2,1)S(1)}, u32[]{:S(2)}, u32[]{:S(2)}) collective-permute-start(f16[32,1024]{1,0:T(8,128)(2,1)S(1)} %fusion.2), channel_id=1, source_target_pairs={{0,3},{1,2},{2,1},{3,0},{4,7},{5,6},{6,5},{7,4},{8,11},{9,10},{10,... | collective-permute-start | bytes 196616 | tf_op jit(solution)/shard_map/ppermute | solution.py:398
  30.5 3.4 %collective-permute-start.7 = (f16[16,1024]{1,0:T(8,128)(2,1)S(1)}, f16[16,1024]{1,0:T(8,128)(2,1)S(1)}, u32[]{:S(2)}, u32[]{:S(2)}) collective-permute-start(f16[16,1024]{1,0:T(8,128)(2,1)S(1)} %slice_convert_fusion), channel_id=1, source_target_pairs={{0,5},{1,4},{2,7},{3,6},{4,1},{5,0},{6,3},{7,2},{8,13},{9,12},{10,... | collective-permute-start | bytes 98312 | tf_op jit(solution)/shard_map/ppermute | solution.py:398
  33.9 4.2 %collective-permute-start.8 = (f16[8,1024]{1,0:T(8,128)(2,1)S(1)}, f16[8,1024]{1,0:T(8,128)(2,1)S(1)}, u32[]{:S(2)}, u32[]{:S(2)}) collective-permute-start(f16[8,1024]{1,0:T(8,128)(2,1)S(1)} %get-tuple-element.39), channel_id=1, source_target_pairs={{0,9},{1,8},{2,11},{3,10},{4,13},{5,12},{6,15},{7,14},{8,1},{9,0},... | collective-permute-start | bytes 49160 | tf_op jit(solution)/shard_map/ppermute | solution.py:398

commit v3 on v2

--- a/solution.py
+++ b/solution.py
@@ -9,9 +9,11 @@
 
 
 DOC_DEV = 8
-CHUNK = 8
+CHUNK = 7
+ROWS = 2 * CHUNK * DOC_DEV
+FURTHER = 4
 GROUP = 8
-UNROLL = 24
+UNROLL = 32
 LOW = -1000000000.0
 SENT = jnp.float16
 SCALE = 4096.0
@@ -34,6 +36,10 @@
     for bit in range(bits):
         out = out ^ ((value >> bit) & 1)
     return out
+
+
+def chunks(value):
+    return (value * 37) >> 8
 
 
 def once(body):
@@ -55,12 +61,13 @@
     extra = jnp.zeros((nb, bl), jnp.int32)
     for slot in range(DOC_DEV):
         n = jnp.sum(jnp.where(doc == slot, livef, 0.0), axis=1, keepdims=True)
-        more = jnp.maximum((n.astype(jnp.int32) - 1) >> 3, 0)
+        more = jnp.maximum(chunks(n.astype(jnp.int32) - 1), 0)
         before = before + jnp.where(doc > slot, n, 0.0)
         extra = extra + jnp.where(doc > slot, more, 0)
     rank = (counted - livef - before).astype(jnp.int32)
-    part, group = rank >> 3, rank & 7
-    row = jnp.where(part == 0, group * 8 + doc, 64 + group * 8 + extra + part - 1)
+    part = chunks(rank)
+    group = rank - part * CHUNK
+    row = group * 8 + jnp.where(part == 0, doc, ROWS // 2 + extra + part - 1)
     return jnp.where(live, row, -1), jnp.where(live, doc, -1)
 
 
@@ -79,13 +86,13 @@
         for u in range(GROUP):
             b = g * GROUP + u
             row = row_ref[start + b : start + b + 1, :]
-            tiles, counts = [], []
+            tiles = []
             for tile in range(2):
                 hits = [
-                    (row == sub + (64 * tile + 8 * i)).astype(jnp.float32) for i in range(CHUNK)
+                    (row == sub + (ROWS // 2 * tile + 8 * i)).astype(jnp.float32)
+                    for i in range(CHUNK)
                 ]
                 count = jnp.sum(functools.reduce(jnp.add, hits), axis=1, keepdims=True)
-                counts.append(count)
                 tiles += hits[:1]
                 tiles += [jnp.where(count > float(i), hits[i], hits[0]) for i in range(1, CHUNK)]
             pick = jnp.concatenate(tiles, axis=0).astype(jnp.bfloat16)
@@ -95,14 +102,14 @@
             doc = doc_ref[start + b : start + b + 1, :]
             n = jnp.sum((doc == sub).astype(jnp.float32), axis=1, keepdims=True)
             n = jnp.broadcast_to(n, (8, dim)).astype(jnp.int32)
-            more = jnp.maximum((n - 1) >> 3, 0)
+            more = jnp.maximum(chunks(n - 1), 0)
             first = jnp.dot(
                 earlier, more.astype(jnp.float32), preferred_element_type=jnp.float32
             ).astype(jnp.int32)
-            for tile in range(2):
-                meta_ref[b, tile] = jnp.broadcast_to((counts[tile] > 0).astype(jnp.int32), (8, dim))
-            for j in range(3):
-                meta_ref[b, 2 + j] = jnp.where(more > j, first + j, 7)
+            meta_ref[b, 0] = n
+            meta_ref[b, 1] = more
+            for j in range(FURTHER):
+                meta_ref[b, 2 + j] = jnp.maximum(jnp.minimum(more - 1, j), 0) + jnp.minimum(first, 7)
 
 
 def vectors_of(h, w):
@@ -176,8 +183,8 @@
 
     def outputs(i):
         shapes = [
-            pltpu.VMEM((sizes[i], 128, dim), jnp.bfloat16),
-            pltpu.VMEM((sizes[i], 5, 8, dim), jnp.int32),
+            pltpu.VMEM((sizes[i], ROWS, dim), jnp.bfloat16),
+            pltpu.VMEM((sizes[i], 2 + FURTHER, 8, dim), jnp.int32),
         ]
         if i + 1 < len(sizes):
             shapes.append(pltpu.VMEM((sizes[i + 1], bl, d), hidden_states.dtype))
@@ -262,11 +269,9 @@
     span = min(columns, 512)
 
     def visit(vec_ref, meta_ref, b, offset, start):
-        apart = owner_ref[offset + b] ^ me
-        place = (parity(apart, bits) << (bits - 1)) | bit_reverse(apart >> 1, bits - 1)
-        rows = pl.ds(pl.multiple_of(place * DOC_DEV, DOC_DEV), DOC_DEV)
+        rows = pl.ds(pl.multiple_of(owner_ref[offset + b] * DOC_DEV, DOC_DEV), DOC_DEV)
         some = [meta_ref[b, tile] > 0 for tile in range(2)]
-        index = [meta_ref[b, 2 + j] for j in range(3)]
+        index = [meta_ref[b, 2 + j] for j in range(FURTHER)]
         tokens = vec_ref[b]
         for t in range(span // width):
             at = pl.ds(start + t * width, width)
@@ -279,16 +284,19 @@
             first, rest = (
                 functools.reduce(
                     jnp.maximum,
-                    [similar[64 * tile + 8 * g : 64 * tile + 8 * g + 8] for g in range(CHUNK)],
+                    [similar[base + 8 * g : base + 8 * g + 8] for g in range(CHUNK)],
                 )
-                for tile in range(2)
+                for base in (0, ROWS // 2)
             )
             best = []
             for c in range(width // 128):
-                top = jnp.where(some[0], first[:, c * 128 : (c + 1) * 128], LOW)
-                further = jnp.where(some[1], rest[:, c * 128 : (c + 1) * 128], LOW)
-                for j in range(3):
-                    top = jnp.maximum(top, jnp.take_along_axis(further, index[j], axis=0))
+                lanes = slice(c * 128, (c + 1) * 128)
+                further = functools.reduce(
+                    jnp.maximum,
+                    [jnp.take_along_axis(rest[:, lanes], at8, axis=0) for at8 in index],
+                )
+                top = jnp.where(some[0], first[:, lanes], LOW)
+                top = jnp.maximum(top, jnp.where(some[1], further, LOW))
                 best.append(top)
             table_ref[rows, at] = jnp.maximum(table_ref[rows, at], jnp.concatenate(best, axis=1))
 
@@ -296,7 +304,7 @@
         offset = 0
         for vec_ref, meta_ref in zip(vec_refs, meta_refs):
             nb = vec_ref.shape[0]
-            step = next(s for s in (UNROLL, 16, 8, 4, 2, 1) if nb % s == 0)
+            step = next(s for s in (UNROLL, 24, 16, 8, 4, 2, 1) if nb % s == 0)
 
             def some_blocks(i, carry, vec_ref=vec_ref, meta_ref=meta_ref, offset=offset, step=step):
                 for u in range(step):
@@ -315,10 +323,14 @@
             return carry
 
         lax.fori_loop(0, columns // span, one_span, 0)
-    half = table_ref.shape[0] // 2
     factor = 1.0 / unit[:1, :1]
-    keep_ref[...] = jnp.maximum(table_ref[:half, :] * factor, NONE)
-    send_ref[...] = jnp.maximum(table_ref[half:, :] * factor, NONE)
+    for place in range(n):
+        high = bit_reverse(place % (n // 2), bits - 1)
+        owner = me ^ (high << 1 | (place // (n // 2) ^ parity(high, bits)))
+        rows = table_ref[pl.ds(pl.multiple_of(owner * DOC_DEV, DOC_DEV), DOC_DEV), :]
+        out_ref = send_ref if place >= n // 2 else keep_ref
+        start = place % (n // 2) * DOC_DEV
+        out_ref[start : start + DOC_DEV, :] = jnp.maximum(rows * factor, NONE)
 
 
 def score(owner, packed, meta, gathered, owners):

time: 39.1 us -> 38.5 us (0.985)
  Pallas kernels: 13.9 us -> 13.4 us
    pallas_call x2, Pallas kernels: 6.65 us -> 5.92 us  [score(): pl.pallas_call(functools.partial(score_kernel, parts=len(packed), pieces=...]
  transfers between devices with their start and end apart: 9 -> 9, of which waited for: 6 -> 6; matrix products, arithmetic and copies ran while one was open for 0% -> 0% of each run, Pallas kernels for 34% -> 33%
where the time goes in v3:
time: 38.5 us; the launch traced here: 38.3 us
  Pallas kernels  13.4 us (35%)
  starting transfers between devices  12.8 us (33%)
  waiting for transfers between devices  11.1 us (29%)
  other arithmetic  0.86 us (2%)
    ppermute x9, starting transfers between devices, swap(): return lax.ppermute(x, 'wide', [(i, i ^ stride) for i in range(n)])  12.8 us
    ppermute x9, waiting for transfers between devices, swap(): return lax.ppermute(x, 'wide', [(i, i ^ stride) for i in range(n)])  11.1 us
    pallas_call x2, Pallas kernels, score(): pl.pallas_call(functools.partial(score_kernel, parts=len(packed), pieces=...  5.92 us
    pallas_call x2, Pallas kernels, following(): pl.pallas_call(functools.partial(pack_next_kernel, start=starts[i], more=...  4.28 us
    pallas_call x1, Pallas kernels, first(): pl.pallas_call(pack_first_kernel, in_specs=[pl.BlockSpec(memory_space=plt...  2.47 us
  transfers between devices with their start and end apart: 9, of which 6 were waited for; matrix products, arithmetic and copies ran while one was open for 0% of the time, Pallas kernels for 33%

profile of v3, /device:TPU:0, one launch (start us, length us, event | category | flops | bytes accessed | tf_op | source)
XLA Modules:
  0.0 38.3 jit_solution(1074593739361316444)
XLA Ops:
  0.0 3.5 %collective-permute-start = (bf16[64,128]{1,0:T(8,128)(2,1)}, bf16[64,128]{1,0:T(8,128)(2,1)S(1)}, u32[]{:S(2)}, u32[]{:S(2)}) collective-permute-start(bf16[64,128]{1,0:T(8,128)(2,1)} %refs_6_.1), channel_id=1, source_target_pairs={{0,9},{1,8},{2,11},{3,10},{4,13},{5,12},{6,15},{7,14},{8,1},{9,0},... | collective-permute-start | bytes 49160 | tf_op jit(solution)/shard_map/ppermute | solution.py:410
  3.5 1.7 %collective-permute-done.refs_7_ = bf16[64,128]{1,0:T(8,128)(2,1)S(1)} collective-permute-done((bf16[64,128]{1,0:T(8,128)(2,1)}, bf16[64,128]{1,0:T(8,128)(2,1)S(1)}, u32[]{:S(2)}, u32[]{:S(2)}) %collective-permute-start) | collective-permute-done | bytes 16416 | tf_op jit(solution)/shard_map/ppermute | solution.py:410
  5.2 0.7 %pad_maximum_fusion.3 = bf16[128,128]{1,0:T(8,128)(2,1)S(1)} fusion(bf16[64,128]{1,0:T(8,128)(2,1)S(1)} %collective-permute-done.refs_7_, bf16[64,128]{1,0:T(8,128)(2,1)} %refs_6_.1), kind=kLoop, calls=%fused_computation.13 | loop fusion | flops 65536 | bytes 65536 | tf_op jit(solution)/shard_map/concatenate | solution.py:417
  5.9 1.9 %collective-permute-start.1 = (bf16[128,128]{1,0:T(8,128)(2,1)S(1)}, bf16[128,128]{1,0:T(8,128)(2,1)S(1)}, u32[]{:S(2)}, u32[]{:S(2)}) collective-permute-start(bf16[128,128]{1,0:T(8,128)(2,1)S(1)} %pad_maximum_fusion.3), channel_id=1, source_target_pairs={{0,5},{1,4},{2,7},{3,6},{4,1},{5,0},{6,3},{7,2},{8,13},{9,12},{10,... | collective-permute-start | bytes 98312 | tf_op jit(solution)/shard_map/ppermute | solution.py:410
  7.8 1.6 %collective-permute-done.1.refs_8_ = bf16[128,128]{1,0:T(8,128)(2,1)S(1)} collective-permute-done((bf16[128,128]{1,0:T(8,128)(2,1)S(1)}, bf16[128,128]{1,0:T(8,128)(2,1)S(1)}, u32[]{:S(2)}, u32[]{:S(2)}) %collective-permute-start.1) | collective-permute-done | bytes 32800 | tf_op jit(solution)/shard_map/ppermute | solution.py:410
  9.4 1.7 %collective-permute-start.2 = (bf16[256,128]{1,0:T(8,128)(2,1)S(1)}, bf16[256,128]{1,0:T(8,128)(2,1)S(1)}, u32[]{:S(2)}, u32[]{:S(2)}) collective-permute-start(bf16[256,128]{1,0:T(8,128)(2,1)S(1)} %pad_maximum_fusion.2), channel_id=1, source_target_pairs={{0,3},{1,2},{2,1},{3,0},{4,7},{5,6},{6,5},{7,4},{8,11},{9,10},{10,... | collective-permute-start | bytes 196616 | tf_op jit(solution)/shard_map/ppermute | solution.py:410
  11.1 2.5 %pack_first.1 = (bf16[8,112,128]{2,1,0:T(8,128)(2,1)S(1)}, s32[8,6,8,128]{3,2,1,0:T(8,128)S(1)}, bf16[24,64,1024]{2,1,0:T(8,128)(2,1)S(1)}, bf16[1024,128]{1,0:T...) custom-call(bf16[64,64,1024]{2,1,0:T(8,128)(2,1)} %refs_0_.1, bf16[1024,128]{1,0:T(8,128)(2,1)} %w_hbm.1, ...), custom_call_target="tpu_custom_call" | custom-call | flops 134217728 | bytes 1048576 | tf_op jit(solution)/shard_map/pack_first/pallas_call | solution.py:205
  13.6 2.2 %pack_next.2 = (bf16[24,112,128]{2,1,0:T(8,128)(2,1)S(1)}, s32[24,6,8,128]{3,2,1,0:T(8,128)S(1)}, bf16[32,64,1024]{2,1,0:T(8,128)(2,1)S(1)}) custom-call(bf16[24,64,1024]{2,1,0:T(8,128)(2,1)S(1)} %get-tuple-element.23.h_ref, bf16[1024,128]{1,0:T(8,128)(2,1)S(1)} %get-tuple-element.24.w_ref, s32[64,64]{1,0:T(8,128)S(1)} %get-tuple-element.25.row_ref, ...), custom_call_target="tpu_custom_call" | custom-call | flops 402653184 | bytes 3145728 | tf_op jit(solution)/shard_map/pack_next/pallas_call | solution.py:223
  15.8 0.0 copy-start
  15.8 0.0 copy-start.1
  15.8 0.0 collective-permute-done.2.refs_9_
  15.9 0.5 %collective-permute-start.3 = (bf16[512,128]{1,0:T(8,128)(2,1)S(1)}, bf16[512,128]{1,0:T(8,128)(2,1)S(1)}, u32[]{:S(2)}, u32[]{:S(2)}) collective-permute-start(bf16[512,128]{1,0:T(8,128)(2,1)S(1)} %pad_maximum_fusion.1), channel_id=1, source_target_pairs={{0,1},{1,0},{2,3},{3,2},{4,5},{5,4},{6,7},{7,6},{8,9},{9,8},{10,11... | collective-permute-start | bytes 393224 | tf_op jit(solution)/shard_map/ppermute | solution.py:410
  16.3 2.1 %pack_next.3 = (bf16[32,112,128]{2,1,0:T(8,128)(2,1)S(1)}, s32[32,6,8,128]{3,2,1,0:T(8,128)S(1)}) custom-call(bf16[32,64,1024]{2,1,0:T(8,128)(2,1)S(1)} %get-tuple-element.28.h_ref, bf16[1024,128]{1,0:T(8,128)(2,1)S(1)} %get-tuple-element.24.w_ref, s32[64,64]{1,0:T(8,128)S(1)} %get-tuple-element.25.row_ref, s32[64,64]{1,0:T(8,128)S(1)} %get-tuple-element.26.doc_ref), custom_call_target="tpu_custom_call" | custom-call | flops 536870912 | bytes 4194304 | tf_op jit(solution)/shard_map/pack_next/pallas_call | solution.py:223
  18.4 0.0 copy-done
  18.4 0.0 copy-done.1
  18.4 3.0 %shard_map.64 = (f32[64,512]{1,0:T(8,128)S(1)}, f32[64,512]{1,0:T(8,128)S(1)}, f32[8,128]{1,0:T(8,128)S(1)}) custom-call(s32[64]{0:T(128)S(1)} %bitcast.1, bf16[8,112,128]{2,1,0:T(8,128)(2,1)S(1)} %get-tuple-element.22.refs_0_, bf16[24,112,128]{2,1,0:T(8,128)(2,1)S(1)} %get-tuple-element.27.refs_1_, bf16[32,112,128]{2,1,0:T(8,128)(2,1)S(1)} %get-tuple-element.29.refs_2_, ...), custom_call_target="tpu_custom_call" | custom-call | flops 939524096 | bytes 3670016 | tf_op jit(solution)/shard_map/pallas_call | solution.py:341
  21.4 0.2 collective-permute-start.5
  21.6 0.0 collective-permute-done.3.refs_6_
  21.6 3.0 %shard_map.65 = (f32[64,512]{1,0:T(8,128)S(1)}, f32[64,512]{1,0:T(8,128)S(1)}, f32[8,128]{1,0:T(8,128)S(1)}) custom-call(s32[64]{0:T(128)S(1)} %bitcast.2, bf16[8,112,128]{2,1,0:T(8,128)(2,1)S(1)} %get-tuple-element.22.refs_0_, bf16[24,112,128]{2,1,0:T(8,128)(2,1)S(1)} %get-tuple-element.27.refs_1_, bf16[32,112,128]{2,1,0:T(8,128)(2,1)S(1)} %get-tuple-element.29.refs_2_, ...), custom_call_target="tpu_custom_call" | custom-call | flops 939524096 | bytes 3670016 | tf_op jit(solution)/shard_map/pallas_call | solution.py:341
  24.6 0.4 %collective-permute-start.4 = (f16[64,512]{1,0:T(8,128)(2,1)S(1)}, f16[64,512]{1,0:T(8,128)(2,1)S(1)}, u32[]{:S(2)}, u32[]{:S(2)}) collective-permute-start(f16[64,512]{1,0:T(8,128)(2,1)S(1)} %convert_element_type.24), channel_id=1, source_target_pairs={{0,1},{1,0},{2,3},{3,2},{4,5},{5,4},{6,7},{7,6},{8,9},{9,8},{10,11... | collective-permute-start | bytes 196616 | tf_op jit(solution)/shard_map/ppermute | solution.py:410
  25.0 0.0 collective-permute-done.5
  25.1 0.9 %collective-permute-done.4 = f16[64,512]{1,0:T(8,128)(2,1)S(1)} collective-permute-done((f16[64,512]{1,0:T(8,128)(2,1)S(1)}, f16[64,512]{1,0:T(8,128)(2,1)S(1)}, u32[]{:S(2)}, u32[]{:S(2)}) %collective-permute-start.4) | collective-permute-done | bytes 65568 | tf_op jit(solution)/shard_map/ppermute | solution.py:410
  26.0 0.2 collective-permute-start.6
  26.2 3.7 %collective-permute-done.6 = f16[32,1024]{1,0:T(8,128)(2,1)S(1)} collective-permute-done((f16[32,1024]{1,0:T(8,128)(2,1)S(1)}, f16[32,1024]{1,0:T(8,128)(2,1)S(1)}, u32[]{:S(2)}, u32[]{:S(2)}) %collective-permute-start.6) | collective-permute-done | bytes 65568 | tf_op jit(solution)/shard_map/ppermute | solution.py:410
  29.9 1.6 %collective-permute-start.7 = (f16[16,1024]{1,0:T(8,128)(2,1)S(1)}, f16[16,1024]{1,0:T(8,128)(2,1)S(1)}, u32[]{:S(2)}, u32[]{:S(2)}) collective-permute-start(f16[16,1024]{1,0:T(8,128)(2,1)S(1)} %slice_convert_fusion), channel_id=1, source_target_pairs={{0,5},{1,4},{2,7},{3,6},{4,1},{5,0},{6,3},{7,2},{8,13},{9,12},{10,... | collective-permute-start | bytes 98312 | tf_op jit(solution)/shard_map/ppermute | solution.py:410
  31.5 1.8 %collective-permute-done.7 = f16[16,1024]{1,0:T(8,128)(2,1)S(1)} collective-permute-done((f16[16,1024]{1,0:T(8,128)(2,1)S(1)}, f16[16,1024]{1,0:T(8,128)(2,1)S(1)}, u32[]{:S(2)}, u32[]{:S(2)}) %collective-permute-start.7) | collective-permute-done | bytes 32800 | tf_op jit(solution)/shard_map/ppermute | solution.py:410
  33.4 2.8 %collective-permute-start.8 = (f16[8,1024]{1,0:T(8,128)(2,1)S(1)}, f16[8,1024]{1,0:T(8,128)(2,1)S(1)}, u32[]{:S(2)}, u32[]{:S(2)}) collective-permute-start(f16[8,1024]{1,0:T(8,128)(2,1)S(1)} %get-tuple-element.39), channel_id=1, source_target_pairs={{0,9},{1,8},{2,11},{3,10},{4,13},{5,12},{6,15},{7,14},{8,1},{9,0},... | collective-permute-start | bytes 49160 | tf_op jit(solution)/shard_map/ppermute | solution.py:410
  36.1 1.4 %collective-permute-done.8 = f16[8,1024]{1,0:T(8,128)(2,1)S(1)} collective-permute-done((f16[8,1024]{1,0:T(8,128)(2,1)S(1)}, f16[8,1024]{1,0:T(8,128)(2,1)S(1)}, u32[]{:S(2)}, u32[]{:S(2)}) %collective-permute-start.8) | collective-permute-done | bytes 16416 | tf_op jit(solution)/shard_map/ppermute | solution.py:410
  37.6 0.7 %finish.1 = f32[8,1024]{1,0:T(8,128)} custom-call(f32[8,1024]{1,0:T(8,128)S(1)} %get-tuple-element.40.keep_ref, f32[8,1024]{1,0:T(8,128)S(1)} %convert_element_type.30.got_ref, f32[8,128]{1,0:T(8,128)S(1)} %get-tuple-element.37.unit_a_ref, f32[8,128]{1,0:T(8,128)S(1)} %get-tuple-element.38.unit_b_ref), custom_call_target="tpu_custom_call" | custom-call | tf_op jit(solution)/shard_map/finish/pallas_call | solution.py:394
  (12 shorter events, 0.1 us)
Async XLA Ops:
  0.0 5.2 %collective-permute-start = (bf16[64,128]{1,0:T(8,128)(2,1)}, bf16[64,128]{1,0:T(8,128)(2,1)S(1)}, u32[]{:S(2)}, u32[]{:S(2)}) collective-permute-start(bf16[64,128]{1,0:T(8,128)(2,1)} %refs_6_.1), channel_id=1, source_target_pairs={{0,9},{1,8},{2,11},{3,10},{4,13},{5,12},{6,15},{7,14},{8,1},{9,0},... | collective-permute-start | bytes 49160 | tf_op jit(solution)/shard_map/ppermute | solution.py:410
  5.9 3.5 %collective-permute-start.1 = (bf16[128,128]{1,0:T(8,128)(2,1)S(1)}, bf16[128,128]{1,0:T(8,128)(2,1)S(1)}, u32[]{:S(2)}, u32[]{:S(2)}) collective-permute-start(bf16[128,128]{1,0:T(8,128)(2,1)S(1)} %pad_maximum_fusion.3), channel_id=1, source_target_pairs={{0,5},{1,4},{2,7},{3,6},{4,1},{5,0},{6,3},{7,2},{8,13},{9,12},{10,... | collective-permute-start | bytes 98312 | tf_op jit(solution)/shard_map/ppermute | solution.py:410
  9.4 6.5 %collective-permute-start.2 = (bf16[256,128]{1,0:T(8,128)(2,1)S(1)}, bf16[256,128]{1,0:T(8,128)(2,1)S(1)}, u32[]{:S(2)}, u32[]{:S(2)}) collective-permute-start(bf16[256,128]{1,0:T(8,128)(2,1)S(1)} %pad_maximum_fusion.2), channel_id=1, source_target_pairs={{0,3},{1,2},{2,1},{3,0},{4,7},{5,6},{6,5},{7,4},{8,11},{9,10},{10,... | collective-permute-start | bytes 196616 | tf_op jit(solution)/shard_map/ppermute | solution.py:410
  15.8 2.6 %copy-start = (bf16[64,128]{1,0:T(8,128)(2,1)S(1)}, bf16[64,128]{1,0:T(8,128)(2,1)}, u32[]{:S(2)}) copy-start(bf16[64,128]{1,0:T(8,128)(2,1)} %refs_6_.1) | copy-start | bytes 49156
  15.8 2.6 %copy-start.1 = (s32[64,1]{0,1:T(1,128)S(1)}, s32[64,1]{0,1:T(1,128)}, u32[]{:S(2)}) copy-start(s32[64,1]{0,1:T(1,128)} %param.7) | copy-start | bytes 772
  15.9 5.7 %collective-permute-start.3 = (bf16[512,128]{1,0:T(8,128)(2,1)S(1)}, bf16[512,128]{1,0:T(8,128)(2,1)S(1)}, u32[]{:S(2)}, u32[]{:S(2)}) collective-permute-start(bf16[512,128]{1,0:T(8,128)(2,1)S(1)} %pad_maximum_fusion.1), channel_id=1, source_target_pairs={{0,1},{1,0},{2,3},{3,2},{4,5},{5,4},{6,7},{7,6},{8,9},{9,8},{10,11... | collective-permute-start | bytes 393224 | tf_op jit(solution)/shard_map/ppermute | solution.py:410
  21.4 3.6 %collective-permute-start.5 = (f16[64,512]{1,0:T(8,128)(2,1)S(1)}, f16[64,512]{1,0:T(8,128)(2,1)S(1)}, u32[]{:S(2)}, u32[]{:S(2)}) collective-permute-start(f16[64,512]{1,0:T(8,128)(2,1)S(1)} %convert_element_type.26), channel_id=1, source_target_pairs={{0,1},{1,0},{2,3},{3,2},{4,5},{5,4},{6,7},{7,6},{8,9},{9,8},{10,11... | collective-permute-start | bytes 196616 | tf_op jit(solution)/shard_map/ppermute | solution.py:410
  24.6 1.3 %collective-permute-start.4 = (f16[64,512]{1,0:T(8,128)(2,1)S(1)}, f16[64,512]{1,0:T(8,128)(2,1)S(1)}, u32[]{:S(2)}, u32[]{:S(2)}) collective-permute-start(f16[64,512]{1,0:T(8,128)(2,1)S(1)} %convert_element_type.24), channel_id=1, source_target_pairs={{0,1},{1,0},{2,3},{3,2},{4,5},{5,4},{6,7},{7,6},{8,9},{9,8},{10,11... | collective-permute-start | bytes 196616 | tf_op jit(solution)/shard_map/ppermute | solution.py:410
  26.0 3.9 %collective-permute-start.6 = (f16[32,1024]{1,0:T(8,128)(2,1)S(1)}, f16[32,1024]{1,0:T(8,128)(2,1)S(1)}, u32[]{:S(2)}, u32[]{:S(2)}) collective-permute-start(f16[32,1024]{1,0:T(8,128)(2,1)S(1)} %fusion.2), channel_id=1, source_target_pairs={{0,3},{1,2},{2,1},{3,0},{4,7},{5,6},{6,5},{7,4},{8,11},{9,10},{10,... | collective-permute-start | bytes 196616 | tf_op jit(solution)/shard_map/ppermute | solution.py:410
  29.9 3.4 %collective-permute-start.7 = (f16[16,1024]{1,0:T(8,128)(2,1)S(1)}, f16[16,1024]{1,0:T(8,128)(2,1)S(1)}, u32[]{:S(2)}, u32[]{:S(2)}) collective-permute-start(f16[16,1024]{1,0:T(8,128)(2,1)S(1)} %slice_convert_fusion), channel_id=1, source_target_pairs={{0,5},{1,4},{2,7},{3,6},{4,1},{5,0},{6,3},{7,2},{8,13},{9,12},{10,... | collective-permute-start | bytes 98312 | tf_op jit(solution)/shard_map/ppermute | solution.py:410
  33.4 4.2 %collective-permute-start.8 = (f16[8,1024]{1,0:T(8,128)(2,1)S(1)}, f16[8,1024]{1,0:T(8,128)(2,1)S(1)}, u32[]{:S(2)}, u32[]{:S(2)}) collective-permute-start(f16[8,1024]{1,0:T(8,128)(2,1)S(1)} %get-tuple-element.39), channel_id=1, source_target_pairs={{0,9},{1,8},{2,11},{3,10},{4,13},{5,12},{6,15},{7,14},{8,1},{9,0},... | collective-permute-start | bytes 49160 | tf_op jit(solution)/shard_map/ppermute | solution.py:410

commit v4 on v3

--- a/solution.py
+++ b/solution.py
@@ -10,6 +10,7 @@
 
 DOC_DEV = 8
 CHUNK = 7
+TOGETHER = 8
 ROWS = 2 * CHUNK * DOC_DEV
 FURTHER = 4
 GROUP = 8
@@ -269,10 +270,7 @@
     span = min(columns, 512)
 
     def visit(vec_ref, meta_ref, b, offset, start):
-        rows = pl.ds(pl.multiple_of(owner_ref[offset + b] * DOC_DEV, DOC_DEV), DOC_DEV)
-        some = [meta_ref[b, tile] > 0 for tile in range(2)]
-        index = [meta_ref[b, 2 + j] for j in range(FURTHER)]
-        tokens = vec_ref[b]
+        tokens = vec_ref[pl.ds(b, TOGETHER)].reshape(TOGETHER * ROWS, -1)
         for t in range(span // width):
             at = pl.ds(start + t * width, width)
             similar = lax.dot_general(
@@ -281,33 +279,38 @@
                 (((1,), (1,)), ((), ())),
                 preferred_element_type=jnp.float32,
             )
-            first, rest = (
-                functools.reduce(
-                    jnp.maximum,
-                    [similar[base + 8 * g : base + 8 * g + 8] for g in range(CHUNK)],
-                )
-                for base in (0, ROWS // 2)
+            for u in range(TOGETHER):
+                merge(similar[u * ROWS : (u + 1) * ROWS], meta_ref, b + u, offset, at)
+
+    def merge(similar, meta_ref, b, offset, at):
+        rows = pl.ds(pl.multiple_of(owner_ref[offset + b] * DOC_DEV, DOC_DEV), DOC_DEV)
+        some = [meta_ref[b, tile] > 0 for tile in range(2)]
+        index = [meta_ref[b, 2 + j] for j in range(FURTHER)]
+        first, rest = (
+            functools.reduce(
+                jnp.maximum,
+                [similar[base + 8 * g : base + 8 * g + 8] for g in range(CHUNK)],
             )
-            best = []
-            for c in range(width // 128):
-                lanes = slice(c * 128, (c + 1) * 128)
-                further = functools.reduce(
-                    jnp.maximum,
-                    [jnp.take_along_axis(rest[:, lanes], at8, axis=0) for at8 in index],
-                )
-                top = jnp.where(some[0], first[:, lanes], LOW)
-                top = jnp.maximum(top, jnp.where(some[1], further, LOW))
-                best.append(top)
-            table_ref[rows, at] = jnp.maximum(table_ref[rows, at], jnp.concatenate(best, axis=1))
+            for base in (0, ROWS // 2)
+        )
+        best = []
+        for c in range(width // 128):
+            lanes = slice(c * 128, (c + 1) * 128)
+            further = functools.reduce(
+                jnp.maximum, [jnp.take_along_axis(rest[:, lanes], at8, axis=0) for at8 in index]
+            )
+            top = jnp.where(some[0], first[:, lanes], LOW)
+            best.append(jnp.maximum(top, jnp.where(some[1], further, LOW)))
+        table_ref[rows, at] = jnp.maximum(table_ref[rows, at], jnp.concatenate(best, axis=1))
 
     def over_blocks(start):
         offset = 0
         for vec_ref, meta_ref in zip(vec_refs, meta_refs):
             nb = vec_ref.shape[0]
-            step = next(s for s in (UNROLL, 24, 16, 8, 4, 2, 1) if nb % s == 0)
+            step = next(s for s in (UNROLL, 24, 16, 8) if nb % s == 0)
 
             def some_blocks(i, carry, vec_ref=vec_ref, meta_ref=meta_ref, offset=offset, step=step):
-                for u in range(step):
+                for u in range(0, step, TOGETHER):
                     visit(vec_ref, meta_ref, i * step + u, offset, start)
                 return carry
 

time: 38.5 us -> 38 us (0.987)
  Pallas kernels: 13.4 us -> 12.9 us
    pallas_call x2, Pallas kernels: 5.92 us -> 5.42 us  [score(): pl.pallas_call(functools.partial(score_kernel, parts=len(packed), pieces=...]
  transfers between devices with their start and end apart: 9 -> 9, of which waited for: 6 -> 6; matrix products, arithmetic and copies ran while one was open for 0% -> 0% of each run, Pallas kernels for 33% -> 32%
where the time goes in v4:
time: 38 us; the launch traced here: 37.8 us
  Pallas kernels  12.9 us (34%)
  starting transfers between devices  12.8 us (34%)
  waiting for transfers between devices  11.1 us (29%)
  other arithmetic  0.86 us (2%)
    ppermute x9, starting transfers between devices, swap(): return lax.ppermute(x, 'wide', [(i, i ^ stride) for i in range(n)])  12.8 us
    ppermute x9, waiting for transfers between devices, swap(): return lax.ppermute(x, 'wide', [(i, i ^ stride) for i in range(n)])  11.1 us
    pallas_call x2, Pallas kernels, score(): pl.pallas_call(functools.partial(score_kernel, parts=len(packed), pieces=...  5.42 us
    pallas_call x2, Pallas kernels, following(): pl.pallas_call(functools.partial(pack_next_kernel, start=starts[i], more=...  4.28 us
    pallas_call x1, Pallas kernels, first(): pl.pallas_call(pack_first_kernel, in_specs=[pl.BlockSpec(memory_space=plt...  2.47 us
  transfers between devices with their start and end apart: 9, of which 6 were waited for; matrix products, arithmetic and copies ran while one was open for 0% of the time, Pallas kernels for 32%

profile of v4, /device:TPU:0, one launch (start us, length us, event | category | flops | bytes accessed | tf_op | source)
XLA Modules:
  0.0 37.8 jit_solution(16048249236360418739)
XLA Ops:
  0.0 3.5 %collective-permute-start = (bf16[64,128]{1,0:T(8,128)(2,1)}, bf16[64,128]{1,0:T(8,128)(2,1)S(1)}, u32[]{:S(2)}, u32[]{:S(2)}) collective-permute-start(bf16[64,128]{1,0:T(8,128)(2,1)} %refs_6_.1), channel_id=1, source_target_pairs={{0,9},{1,8},{2,11},{3,10},{4,13},{5,12},{6,15},{7,14},{8,1},{9,0},... | collective-permute-start | bytes 49160 | tf_op jit(solution)/shard_map/ppermute | solution.py:413
  3.5 1.7 %collective-permute-done.refs_7_ = bf16[64,128]{1,0:T(8,128)(2,1)S(1)} collective-permute-done((bf16[64,128]{1,0:T(8,128)(2,1)}, bf16[64,128]{1,0:T(8,128)(2,1)S(1)}, u32[]{:S(2)}, u32[]{:S(2)}) %collective-permute-start) | collective-permute-done | bytes 16416 | tf_op jit(solution)/shard_map/ppermute | solution.py:413
  5.2 0.7 %pad_maximum_fusion.3 = bf16[128,128]{1,0:T(8,128)(2,1)S(1)} fusion(bf16[64,128]{1,0:T(8,128)(2,1)S(1)} %collective-permute-done.refs_7_, bf16[64,128]{1,0:T(8,128)(2,1)} %refs_6_.1), kind=kLoop, calls=%fused_computation.13 | loop fusion | flops 65536 | bytes 65536 | tf_op jit(solution)/shard_map/concatenate | solution.py:420
  5.9 1.9 %collective-permute-start.1 = (bf16[128,128]{1,0:T(8,128)(2,1)S(1)}, bf16[128,128]{1,0:T(8,128)(2,1)S(1)}, u32[]{:S(2)}, u32[]{:S(2)}) collective-permute-start(bf16[128,128]{1,0:T(8,128)(2,1)S(1)} %pad_maximum_fusion.3), channel_id=1, source_target_pairs={{0,5},{1,4},{2,7},{3,6},{4,1},{5,0},{6,3},{7,2},{8,13},{9,12},{10,... | collective-permute-start | bytes 98312 | tf_op jit(solution)/shard_map/ppermute | solution.py:413
  7.8 1.6 %collective-permute-done.1.refs_8_ = bf16[128,128]{1,0:T(8,128)(2,1)S(1)} collective-permute-done((bf16[128,128]{1,0:T(8,128)(2,1)S(1)}, bf16[128,128]{1,0:T(8,128)(2,1)S(1)}, u32[]{:S(2)}, u32[]{:S(2)}) %collective-permute-start.1) | collective-permute-done | bytes 32800 | tf_op jit(solution)/shard_map/ppermute | solution.py:413
  9.4 1.7 %collective-permute-start.2 = (bf16[256,128]{1,0:T(8,128)(2,1)S(1)}, bf16[256,128]{1,0:T(8,128)(2,1)S(1)}, u32[]{:S(2)}, u32[]{:S(2)}) collective-permute-start(bf16[256,128]{1,0:T(8,128)(2,1)S(1)} %pad_maximum_fusion.2), channel_id=1, source_target_pairs={{0,3},{1,2},{2,1},{3,0},{4,7},{5,6},{6,5},{7,4},{8,11},{9,10},{10,... | collective-permute-start | bytes 196616 | tf_op jit(solution)/shard_map/ppermute | solution.py:413
  11.1 2.5 %pack_first.1 = (bf16[8,112,128]{2,1,0:T(8,128)(2,1)S(1)}, s32[8,6,8,128]{3,2,1,0:T(8,128)S(1)}, bf16[24,64,1024]{2,1,0:T(8,128)(2,1)S(1)}, bf16[1024,128]{1,0:T...) custom-call(bf16[64,64,1024]{2,1,0:T(8,128)(2,1)} %refs_0_.1, bf16[1024,128]{1,0:T(8,128)(2,1)} %w_hbm.1, ...), custom_call_target="tpu_custom_call" | custom-call | flops 134217728 | bytes 1048576 | tf_op jit(solution)/shard_map/pack_first/pallas_call | solution.py:206
  13.6 2.2 %pack_next.2 = (bf16[24,112,128]{2,1,0:T(8,128)(2,1)S(1)}, s32[24,6,8,128]{3,2,1,0:T(8,128)S(1)}, bf16[32,64,1024]{2,1,0:T(8,128)(2,1)S(1)}) custom-call(bf16[24,64,1024]{2,1,0:T(8,128)(2,1)S(1)} %get-tuple-element.23.h_ref, bf16[1024,128]{1,0:T(8,128)(2,1)S(1)} %get-tuple-element.24.w_ref, s32[64,64]{1,0:T(8,128)S(1)} %get-tuple-element.25.row_ref, ...), custom_call_target="tpu_custom_call" | custom-call | flops 402653184 | bytes 3145728 | tf_op jit(solution)/shard_map/pack_next/pallas_call | solution.py:224
  15.8 0.0 copy-start
  15.8 0.0 copy-start.1
  15.8 0.0 collective-permute-done.2.refs_9_
  15.9 0.5 %collective-permute-start.3 = (bf16[512,128]{1,0:T(8,128)(2,1)S(1)}, bf16[512,128]{1,0:T(8,128)(2,1)S(1)}, u32[]{:S(2)}, u32[]{:S(2)}) collective-permute-start(bf16[512,128]{1,0:T(8,128)(2,1)S(1)} %pad_maximum_fusion.1), channel_id=1, source_target_pairs={{0,1},{1,0},{2,3},{3,2},{4,5},{5,4},{6,7},{7,6},{8,9},{9,8},{10,11... | collective-permute-start | bytes 393224 | tf_op jit(solution)/shard_map/ppermute | solution.py:413
  16.3 2.1 %pack_next.3 = (bf16[32,112,128]{2,1,0:T(8,128)(2,1)S(1)}, s32[32,6,8,128]{3,2,1,0:T(8,128)S(1)}) custom-call(bf16[32,64,1024]{2,1,0:T(8,128)(2,1)S(1)} %get-tuple-element.28.h_ref, bf16[1024,128]{1,0:T(8,128)(2,1)S(1)} %get-tuple-element.24.w_ref, s32[64,64]{1,0:T(8,128)S(1)} %get-tuple-element.25.row_ref, s32[64,64]{1,0:T(8,128)S(1)} %get-tuple-element.26.doc_ref), custom_call_target="tpu_custom_call" | custom-call | flops 536870912 | bytes 4194304 | tf_op jit(solution)/shard_map/pack_next/pallas_call | solution.py:224
  18.4 0.0 copy-done
  18.4 0.0 copy-done.1
  18.4 2.7 %shard_map.64 = (f32[64,512]{1,0:T(8,128)S(1)}, f32[64,512]{1,0:T(8,128)S(1)}, f32[8,128]{1,0:T(8,128)S(1)}) custom-call(s32[64]{0:T(128)S(1)} %bitcast.1, bf16[8,112,128]{2,1,0:T(8,128)(2,1)S(1)} %get-tuple-element.22.refs_0_, bf16[24,112,128]{2,1,0:T(8,128)(2,1)S(1)} %get-tuple-element.27.refs_1_, bf16[32,112,128]{2,1,0:T(8,128)(2,1)S(1)} %get-tuple-element.29.refs_2_, ...), custom_call_target="tpu_custom_call" | custom-call | flops 939524096 | bytes 3670016 | tf_op jit(solution)/shard_map/pallas_call | solution.py:344
  21.1 0.2 collective-permute-start.5
  21.3 0.0 collective-permute-done.3.refs_6_
  21.3 2.7 %shard_map.65 = (f32[64,512]{1,0:T(8,128)S(1)}, f32[64,512]{1,0:T(8,128)S(1)}, f32[8,128]{1,0:T(8,128)S(1)}) custom-call(s32[64]{0:T(128)S(1)} %bitcast.2, bf16[8,112,128]{2,1,0:T(8,128)(2,1)S(1)} %get-tuple-element.22.refs_0_, bf16[24,112,128]{2,1,0:T(8,128)(2,1)S(1)} %get-tuple-element.27.refs_1_, bf16[32,112,128]{2,1,0:T(8,128)(2,1)S(1)} %get-tuple-element.29.refs_2_, ...), custom_call_target="tpu_custom_call" | custom-call | flops 939524096 | bytes 3670016 | tf_op jit(solution)/shard_map/pallas_call | solution.py:344
  24.1 0.4 %collective-permute-start.4 = (f16[64,512]{1,0:T(8,128)(2,1)S(1)}, f16[64,512]{1,0:T(8,128)(2,1)S(1)}, u32[]{:S(2)}, u32[]{:S(2)}) collective-permute-start(f16[64,512]{1,0:T(8,128)(2,1)S(1)} %convert_element_type.24), channel_id=1, source_target_pairs={{0,1},{1,0},{2,3},{3,2},{4,5},{5,4},{6,7},{7,6},{8,9},{9,8},{10,11... | collective-permute-start | bytes 196616 | tf_op jit(solution)/shard_map/ppermute | solution.py:413
  24.5 0.0 collective-permute-done.5
  24.6 0.9 %collective-permute-done.4 = f16[64,512]{1,0:T(8,128)(2,1)S(1)} collective-permute-done((f16[64,512]{1,0:T(8,128)(2,1)S(1)}, f16[64,512]{1,0:T(8,128)(2,1)S(1)}, u32[]{:S(2)}, u32[]{:S(2)}) %collective-permute-start.4) | collective-permute-done | bytes 65568 | tf_op jit(solution)/shard_map/ppermute | solution.py:413
  25.5 0.2 collective-permute-start.6
  25.7 3.7 %collective-permute-done.6 = f16[32,1024]{1,0:T(8,128)(2,1)S(1)} collective-permute-done((f16[32,1024]{1,0:T(8,128)(2,1)S(1)}, f16[32,1024]{1,0:T(8,128)(2,1)S(1)}, u32[]{:S(2)}, u32[]{:S(2)}) %collective-permute-start.6) | collective-permute-done | bytes 65568 | tf_op jit(solution)/shard_map/ppermute | solution.py:413
  29.4 1.6 %collective-permute-start.7 = (f16[16,1024]{1,0:T(8,128)(2,1)S(1)}, f16[16,1024]{1,0:T(8,128)(2,1)S(1)}, u32[]{:S(2)}, u32[]{:S(2)}) collective-permute-start(f16[16,1024]{1,0:T(8,128)(2,1)S(1)} %slice_convert_fusion), channel_id=1, source_target_pairs={{0,5},{1,4},{2,7},{3,6},{4,1},{5,0},{6,3},{7,2},{8,13},{9,12},{10,... | collective-permute-start | bytes 98312 | tf_op jit(solution)/shard_map/ppermute | solution.py:413
  31.0 1.8 %collective-permute-done.7 = f16[16,1024]{1,0:T(8,128)(2,1)S(1)} collective-permute-done((f16[16,1024]{1,0:T(8,128)(2,1)S(1)}, f16[16,1024]{1,0:T(8,128)(2,1)S(1)}, u32[]{:S(2)}, u32[]{:S(2)}) %collective-permute-start.7) | collective-permute-done | bytes 32800 | tf_op jit(solution)/shard_map/ppermute | solution.py:413
  32.9 2.8 %collective-permute-start.8 = (f16[8,1024]{1,0:T(8,128)(2,1)S(1)}, f16[8,1024]{1,0:T(8,128)(2,1)S(1)}, u32[]{:S(2)}, u32[]{:S(2)}) collective-permute-start(f16[8,1024]{1,0:T(8,128)(2,1)S(1)} %get-tuple-element.39), channel_id=1, source_target_pairs={{0,9},{1,8},{2,11},{3,10},{4,13},{5,12},{6,15},{7,14},{8,1},{9,0},... | collective-permute-start | bytes 49160 | tf_op jit(solution)/shard_map/ppermute | solution.py:413
  35.6 1.4 %collective-permute-done.8 = f16[8,1024]{1,0:T(8,128)(2,1)S(1)} collective-permute-done((f16[8,1024]{1,0:T(8,128)(2,1)S(1)}, f16[8,1024]{1,0:T(8,128)(2,1)S(1)}, u32[]{:S(2)}, u32[]{:S(2)}) %collective-permute-start.8) | collective-permute-done | bytes 16416 | tf_op jit(solution)/shard_map/ppermute | solution.py:413
  37.1 0.7 %finish.1 = f32[8,1024]{1,0:T(8,128)} custom-call(f32[8,1024]{1,0:T(8,128)S(1)} %get-tuple-element.40.keep_ref, f32[8,1024]{1,0:T(8,128)S(1)} %convert_element_type.30.got_ref, f32[8,128]{1,0:T(8,128)S(1)} %get-tuple-element.37.unit_a_ref, f32[8,128]{1,0:T(8,128)S(1)} %get-tuple-element.38.unit_b_ref), custom_call_target="tpu_custom_call" | custom-call | tf_op jit(solution)/shard_map/finish/pallas_call | solution.py:397
  (12 shorter events, 0.1 us)
Async XLA Ops:
  0.0 5.2 %collective-permute-start = (bf16[64,128]{1,0:T(8,128)(2,1)}, bf16[64,128]{1,0:T(8,128)(2,1)S(1)}, u32[]{:S(2)}, u32[]{:S(2)}) collective-permute-start(bf16[64,128]{1,0:T(8,128)(2,1)} %refs_6_.1), channel_id=1, source_target_pairs={{0,9},{1,8},{2,11},{3,10},{4,13},{5,12},{6,15},{7,14},{8,1},{9,0},... | collective-permute-start | bytes 49160 | tf_op jit(solution)/shard_map/ppermute | solution.py:413
  5.9 3.5 %collective-permute-start.1 = (bf16[128,128]{1,0:T(8,128)(2,1)S(1)}, bf16[128,128]{1,0:T(8,128)(2,1)S(1)}, u32[]{:S(2)}, u32[]{:S(2)}) collective-permute-start(bf16[128,128]{1,0:T(8,128)(2,1)S(1)} %pad_maximum_fusion.3), channel_id=1, source_target_pairs={{0,5},{1,4},{2,7},{3,6},{4,1},{5,0},{6,3},{7,2},{8,13},{9,12},{10,... | collective-permute-start | bytes 98312 | tf_op jit(solution)/shard_map/ppermute | solution.py:413
  9.4 6.5 %collective-permute-start.2 = (bf16[256,128]{1,0:T(8,128)(2,1)S(1)}, bf16[256,128]{1,0:T(8,128)(2,1)S(1)}, u32[]{:S(2)}, u32[]{:S(2)}) collective-permute-start(bf16[256,128]{1,0:T(8,128)(2,1)S(1)} %pad_maximum_fusion.2), channel_id=1, source_target_pairs={{0,3},{1,2},{2,1},{3,0},{4,7},{5,6},{6,5},{7,4},{8,11},{9,10},{10,... | collective-permute-start | bytes 196616 | tf_op jit(solution)/shard_map/ppermute | solution.py:413
  15.8 2.6 %copy-start = (bf16[64,128]{1,0:T(8,128)(2,1)S(1)}, bf16[64,128]{1,0:T(8,128)(2,1)}, u32[]{:S(2)}) copy-start(bf16[64,128]{1,0:T(8,128)(2,1)} %refs_6_.1) | copy-start | bytes 49156
  15.8 2.6 %copy-start.1 = (s32[64,1]{0,1:T(1,128)S(1)}, s32[64,1]{0,1:T(1,128)}, u32[]{:S(2)}) copy-start(s32[64,1]{0,1:T(1,128)} %param.7) | copy-start | bytes 772
  15.9 5.5 %collective-permute-start.3 = (bf16[512,128]{1,0:T(8,128)(2,1)S(1)}, bf16[512,128]{1,0:T(8,128)(2,1)S(1)}, u32[]{:S(2)}, u32[]{:S(2)}) collective-permute-start(bf16[512,128]{1,0:T(8,128)(2,1)S(1)} %pad_maximum_fusion.1), channel_id=1, source_target_pairs={{0,1},{1,0},{2,3},{3,2},{4,5},{5,4},{6,7},{7,6},{8,9},{9,8},{10,11... | collective-permute-start | bytes 393224 | tf_op jit(solution)/shard_map/ppermute | solution.py:413
  21.1 3.4 %collective-permute-start.5 = (f16[64,512]{1,0:T(8,128)(2,1)S(1)}, f16[64,512]{1,0:T(8,128)(2,1)S(1)}, u32[]{:S(2)}, u32[]{:S(2)}) collective-permute-start(f16[64,512]{1,0:T(8,128)(2,1)S(1)} %convert_element_type.26), channel_id=1, source_target_pairs={{0,1},{1,0},{2,3},{3,2},{4,5},{5,4},{6,7},{7,6},{8,9},{9,8},{10,11... | collective-permute-start | bytes 196616 | tf_op jit(solution)/shard_map/ppermute | solution.py:413
  24.1 1.4 %collective-permute-start.4 = (f16[64,512]{1,0:T(8,128)(2,1)S(1)}, f16[64,512]{1,0:T(8,128)(2,1)S(1)}, u32[]{:S(2)}, u32[]{:S(2)}) collective-permute-start(f16[64,512]{1,0:T(8,128)(2,1)S(1)} %convert_element_type.24), channel_id=1, source_target_pairs={{0,1},{1,0},{2,3},{3,2},{4,5},{5,4},{6,7},{7,6},{8,9},{9,8},{10,11... | collective-permute-start | bytes 196616 | tf_op jit(solution)/shard_map/ppermute | solution.py:413
  25.5 3.9 %collective-permute-start.6 = (f16[32,1024]{1,0:T(8,128)(2,1)S(1)}, f16[32,1024]{1,0:T(8,128)(2,1)S(1)}, u32[]{:S(2)}, u32[]{:S(2)}) collective-permute-start(f16[32,1024]{1,0:T(8,128)(2,1)S(1)} %fusion.2), channel_id=1, source_target_pairs={{0,3},{1,2},{2,1},{3,0},{4,7},{5,6},{6,5},{7,4},{8,11},{9,10},{10,... | collective-permute-start | bytes 196616 | tf_op jit(solution)/shard_map/ppermute | solution.py:413
  29.4 3.4 %collective-permute-start.7 = (f16[16,1024]{1,0:T(8,128)(2,1)S(1)}, f16[16,1024]{1,0:T(8,128)(2,1)S(1)}, u32[]{:S(2)}, u32[]{:S(2)}) collective-permute-start(f16[16,1024]{1,0:T(8,128)(2,1)S(1)} %slice_convert_fusion), channel_id=1, source_target_pairs={{0,5},{1,4},{2,7},{3,6},{4,1},{5,0},{6,3},{7,2},{8,13},{9,12},{10,... | collective-permute-start | bytes 98312 | tf_op jit(solution)/shard_map/ppermute | solution.py:413
  32.9 4.2 %collective-permute-start.8 = (f16[8,1024]{1,0:T(8,128)(2,1)S(1)}, f16[8,1024]{1,0:T(8,128)(2,1)S(1)}, u32[]{:S(2)}, u32[]{:S(2)}) collective-permute-start(f16[8,1024]{1,0:T(8,128)(2,1)S(1)} %get-tuple-element.39), channel_id=1, source_target_pairs={{0,9},{1,8},{2,11},{3,10},{4,13},{5,12},{6,15},{7,14},{8,1},{9,0},... | collective-permute-start | bytes 49160 | tf_op jit(solution)/shard_map/ppermute | solution.py:413
